TPU v7x, 32 devices: a whole 2x2x4 slice. The times are simulated.
32 devices in a mesh: parts: 2 (over y), seq: 16 (over z, x, core).
Axes of the slice: x: 2, y: 2, z: 4, core: 2. Of those that a mesh axis runs over, the one named last changes fastest.
Arguments:
- ids: int32 [8192], P(('parts', 'seq')), parts along dimension 0, may hold values from 0 to 15
- exponents: int32 [16, 8192], P(None, ('parts', 'seq')), parts along dimension 1, may hold values from 1 to 8192
- embedding: bfloat16 [16, 1024], replicated, may hold values from -6 to 6
- norm_gain: float32 [1024], replicated, may hold values from 0.5 to 1.5
- in_proj: bfloat16 [1024, 2304], replicated, may hold values from -0.1875 to 0.1875
- conv_weight: float32 [2, 4, 1280], replicated, may hold values from -3 to 3
- conv_bias: float32 [2, 1280], replicated, may hold values from -3 to 3
- rates: float32 [2, 16], replicated, may hold values from 2.4414063e-05 to 0.016666667
- head_gain: float32 [2, 1024], replicated, may hold values from 0.25 to 1.75
- out_proj: bfloat16 [1024, 1024], replicated, may hold values from -0.125 to 0.125
Outputs:
- mixed: bfloat16 [8192, 1024], P(('parts', 'seq')), parts along dimension 0
There are 2 independent parts, one for each index of `parts`. A program takes and returns all parts, laid end to end along the dimension named above; an argument that names none is the same for every part. Nothing has to cross between parts.
All inputs are finite; a program needn't handle non-finite values.
Results may differ from a plain program's by a relative error of at most 0.0071.
Values may be sent and summed in bfloat16 or wider, within the bound.
No kernel may reach another device: no remote copies, remote signals or barrier semaphores. Data moves between devices by JAX's collectives and lax.ppermute only.
A program may use at most 384 MiB of HBM per device.

v0:
```python
import functools

import jax
import jax.numpy as jnp
from jax import lax
from jax.experimental import pallas as pl
from jax.experimental.pallas import tpu as pltpu
from jax.sharding import PartitionSpec as P

EPS = 1e-05
LOG2E = 1.4426950408889634
F32 = jnp.float32
BF16 = jnp.bfloat16
NT = (((1,), (1,)), ((), ()))
TN = (((0,), (0,)), ((), ()))
VMEM_LIMIT = 56 * 1024 * 1024


def dot(a, b, dims=(((1,), (0,)), ((), ()))):
    return lax.dot_general(a, b, dims, preferred_element_type=F32)


def split(value):
    high = value.astype(BF16)
    return high, (value - high.astype(F32)).astype(BF16)


def tables_kernel(emb_ref, gain_ref, in_ref, cw_ref, cb_ref, hg_ref, conv_ref, gate_ref, hgt_ref):
    vocab = emb_ref.shape[0]
    inner = hg_ref.shape[1]
    wide = cw_ref.shape[2]
    taps = cw_ref.shape[1]
    e = emb_ref[...].astype(F32)
    norm = e * lax.rsqrt(jnp.mean(e * e, axis=1, keepdims=True) + EPS) * gain_ref[...]
    norm = norm.astype(BF16)
    gate = dot(norm, in_ref[:, :inner]).astype(BF16).astype(F32)
    gate = gate / (1.0 + jnp.exp(-gate))
    g0 = gate.astype(BF16)
    g1, g2 = split(gate - g0.astype(F32))
    pad = jnp.zeros((gate_ref.shape[1] - 3 * vocab, inner), BF16)
    gate_ref[...] = jnp.concatenate([g0, g1, g2, pad], axis=0).T
    proj = dot(norm, in_ref[:, inner:]).astype(BF16).astype(F32)
    for b in range(2):
        rows = []
        for j in range(taps):
            row = cw_ref[b, j : j + 1, :] * proj
            if j == taps - 1:
                row = row + cb_ref[b : b + 1, :]
            rows.append(0.5 * row)
        high, low = split(jnp.concatenate(rows, axis=0))
        conv_ref[b] = jnp.concatenate([high, low], axis=0).T
    hg = jnp.concatenate([hg_ref[...], jnp.zeros((126, inner), F32)], axis=0)
    hgt_ref[...] = hg.T


def mixer_kernel(
    count, bits,
    me_ref, rates_ref, data_ref, conv_ref, gate_ref, hgt_ref, out_proj_ref,
    mixed_ref,
    expo, within, total, ids, shifted, state, mixin,
):
    heads, span = data_ref.shape[1], data_ref.shape[2]
    inner = out_proj_ref.shape[0]
    head = inner // heads
    wide = conv_ref.shape[1]
    width = (wide - inner) // 2
    vocab = conv_ref.shape[2] // 8
    me = me_ref[0]

    def unpack(c, _):
        away = jnp.bitwise_xor(me, c)
        slot = jnp.int32(0)
        for i in range(bits):
            slot = slot + (((away >> i) & 1) << (bits - 1 - i))
        raw = data_ref[slot]
        expo[c] = (raw & 0xFFFF) + 1
        ids[pl.ds(c, 1), :] = raw[0:1] >> 16
        return 0

    for c in range(count) if count <= 32 else ():
        unpack(c, 0)
    if count > 32:
        lax.fori_loop(0, count, unpack, 0)

    e = expo[...].reshape(count * heads, span)
    lower = lax.broadcasted_iota(jnp.int32, (span, span), 0)
    upper = lax.broadcasted_iota(jnp.int32, (span, span), 1)
    before = jnp.where(lower < upper, 1.0, 0.0).astype(BF16)
    pre = 256.0 * dot((e >> 8).astype(F32).astype(BF16), before) + dot(
        (e & 255).astype(F32).astype(BF16), before
    )
    within[0] = pre.reshape(count, heads, span)
    inc = pre + e.astype(F32)
    tot = jnp.broadcast_to(inc[:, span - 1 :], inc.shape)
    total[...] = tot.reshape(count, heads, span)
    within[1] = (tot - inc).reshape(count, heads, span)

    tok = ids[...]
    lane = lax.broadcasted_iota(jnp.int32, tok.shape, 1)
    row = lax.broadcasted_iota(jnp.int32, tok.shape, 0)
    for d in range(-3, 4):
        if d == 0:
            moved = tok
        elif d < 0:
            here = pltpu.roll(tok, -d, axis=1)
            other = jnp.where(row == 0, -1, pltpu.roll(here, 1, axis=0))
            moved = jnp.where(lane < -d, other, here)
        else:
            here = pltpu.roll(tok, span - d, axis=1)
            other = jnp.where(row == count - 1, -1, pltpu.roll(here, count - 1, axis=0))
            moved = jnp.where(lane >= span - d, other, here)
        shifted[d + 3] = moved

    values = lax.broadcasted_iota(jnp.int32, (vocab, span), 0)

    def onehot(c, sign):
        rows = []
        for j in range(4):
            token = shifted[3 + (j - 3) * sign, pl.ds(c, 1), :]
            rows.append(jnp.where(values == token, 1.0, 0.0))
        one = jnp.concatenate(rows, axis=0).astype(BF16)
        return jnp.concatenate([one, one], axis=0)

    def convolve(table, one):
        half = dot(table, one)
        return half + half * jnp.tanh(half)

    def rate_of(b, value):
        col = [rates_ref[b, h] * value[h : h + 1] for h in range(heads)]
        return jnp.concatenate(col, axis=0)

    state[...] = jnp.zeros_like(state)

    def remote(i, run):
        rev = i >= me
        b = rev.astype(jnp.int32)
        c = jnp.where(rev, i + 1, me - 1 - i)
        run = jnp.where(i == me, 0.0, run)
        dist = within[1 - b, c] + run
        decay = jnp.exp(-rate_of(b, dist))
        one = onehot(c, 1 - 2 * b)
        x = convolve(conv_ref[b, :inner, :], one)
        x = x.reshape(heads, head, span) * decay[:, None, :]
        x = x.reshape(inner, span).astype(BF16)
        bt = convolve(conv_ref[b, inner : inner + width, :], one).astype(BF16)
        state[b] += dot(x, bt, NT)
        return run + total[c]

    lax.fori_loop(0, count - 1, remote, jnp.zeros((heads, span), F32))

    own_pre = within[0, me]
    own_inc = own_pre + expo[me].astype(F32)
    own_tot = total[me]
    current = jnp.where(values == ids[pl.ds(me, 1), :], 1.0, 0.0).astype(BF16)
    current = jnp.concatenate(
        [current] * 3 + [jnp.zeros((gate_ref.shape[1] - 3 * vocab, span), BF16)], axis=0
    )
    gates = dot(gate_ref[...], current)
    for b in range(2):
        one = onehot(me, 1 - 2 * b)
        conv = convolve(conv_ref[b], one).astype(BF16)
        xt = conv[:inner]
        bt = conv[inner : inner + width]
        ct = conv[inner + width :]
        scores = dot(bt, ct, TN)
        cum = own_inc if b == 0 else own_pre
        cum_col = cum.T
        reach = own_inc if b == 0 else own_tot - own_pre
        high, low = split(state[b])
        carried = dot(
            jnp.concatenate([high, low], axis=1), jnp.concatenate([ct, ct], axis=0)
        )
        keep = lower <= upper if b == 0 else lower >= upper
        for h in range(heads):
            rows = slice(h * head, (h + 1) * head)
            rate = rates_ref[b, h]
            gap = cum[h : h + 1] - cum_col[:, h : h + 1]
            factor = -LOG2E if b == 0 else LOG2E
            w = jnp.where(keep, scores * jnp.exp2(gap * (rate * factor)), 0.0).astype(BF16)
            y = dot(xt[rows], w)
            y = y + jnp.exp(-rate * reach[h : h + 1]) * carried[rows]
            v = y * gates[rows]
            inv = lax.rsqrt(jnp.sum(v * v, axis=0, keepdims=True) * (1.0 / head) + EPS)
            out = v * inv * hgt_ref[rows, b : b + 1]
            if b == 0:
                mixin[rows] = out
            else:
                mixin[rows] = mixin[rows] + out
    mixed_ref[...] = dot(mixin[...].astype(BF16), out_proj_ref[...], TN).astype(BF16)


def shards(
    ids, exponents, embedding, norm_gain, in_proj, conv_weight, conv_bias, rates, head_gain, out_proj
):
    count = lax.axis_size("seq")
    me = lax.axis_index("seq")
    bits = count.bit_length() - 1
    heads, span = exponents.shape
    vocab = embedding.shape[0]
    inner = out_proj.shape[0]
    wide = conv_bias.shape[1]
    width = (wide - inner) // 2
    taps = conv_weight.shape[1]
    params = pltpu.CompilerParams(vmem_limit_bytes=VMEM_LIMIT)
    vmem = pl.BlockSpec(memory_space=pltpu.VMEM)
    smem = pl.BlockSpec(memory_space=pltpu.SMEM)

    conv_table, gate_table, gain_table = pl.pallas_call(
        tables_kernel,
        out_shape=(
            jax.ShapeDtypeStruct((2, wide, 2 * taps * vocab), BF16),
            jax.ShapeDtypeStruct((inner, 128), BF16),
            jax.ShapeDtypeStruct((inner, 128), F32),
        ),
        in_specs=[vmem] * 6,
        out_specs=(vmem, vmem, vmem),
        compiler_params=params,
        name="tables",
        cost_estimate=pl.CostEstimate(flops=80_000_000, bytes_accessed=6_000_000, transcendentals=16384),
    )(embedding, norm_gain[None, :], in_proj, conv_weight, conv_bias, head_gain)

    held = ((exponents - 1) + (ids << 16)[None, :])[None]
    for bit in reversed(range(bits)):
        far = 1 << bit
        other = lax.ppermute(held, "seq", [(i, i ^ far) for i in range(count)])
        held = jnp.concatenate([held, other], axis=0)

    return pl.pallas_call(
        functools.partial(mixer_kernel, count, bits),
        out_shape=jax.ShapeDtypeStruct((span, inner), BF16),
        in_specs=[smem, smem] + [vmem] * 5,
        out_specs=vmem,
        scratch_shapes=[
            pltpu.VMEM((count, heads, span), jnp.int32),
            pltpu.VMEM((2, count, heads, span), F32),
            pltpu.VMEM((count, heads, span), F32),
            pltpu.VMEM((count, span), jnp.int32),
            pltpu.VMEM((7, count, span), jnp.int32),
            pltpu.VMEM((2, inner, width), F32),
            pltpu.VMEM((inner, span), F32),
        ],
        compiler_params=params,
        name="mixer",
        cost_estimate=pl.CostEstimate(flops=12_000_000_000, bytes_accessed=6_000_000, transcendentals=8_000_000),
    )(me[None].astype(jnp.int32), rates, held, conv_table, gate_table, gain_table, out_proj)


def solution(mesh):
    in_specs = (
        P(("parts", "seq")),
        P(None, ("parts", "seq")),
        P(), P(), P(), P(), P(), P(), P(), P(),
    )
    out_specs = P(("parts", "seq"), None)
    return jax.shard_map(shards, mesh=mesh, in_specs=in_specs, out_specs=out_specs, check_vma=False)
```

profile of v0, /device:TPU:0, one launch (start us, length us, event | category | flops | bytes accessed | tf_op | source)
XLA Modules:
  0.0 35.1 jit_solution(10386845373160889143)
XLA Ops:
  0.0 0.7 %broadcast_shift-left_fusion = s32[256]{0:T(256)S(1)} fusion(s32[256]{0:T(256)} %param.10), kind=kLoop, calls=%fused_computation.9 | loop fusion | flops 256 | bytes 2048 | tf_op jit(solution)/shard_map/shift_left | solution.py:222
  0.7 0.7 %constant_dynamic-update-slice_fusion.4 = (s32[16,16,256]{2,1,0:T(8,128)S(1)}, s32[1,16,256]{2,1,0:T(8,128)S(1)}) fusion(s32[256]{0:T(256)S(1)} %broadcast_shift-left_fusion, s32[16,256]{1,0:T(8,128)} %param.11), kind=kLoop, calls=%fused_computation.8 | loop fusion | flops 8191 | bytes 50176
  1.4 4.0 %collective-permute-start = (s32[1,16,256]{2,1,0:T(8,128)S(1)}, s32[1,16,256]{2,1,0:T(8,128)S(1)}, u32[]{:S(2)}, u32[]{:S(2)}) collective-permute-start(s32[1,16,256]{2,1,0:T(8,128)S(1)} %get-tuple-element.12), channel_id=1, source_target_pairs={{0,8},{1,9},{2,10},{3,11},{4,12},{5,13},{6,14},{7,15},{8,0},{9,1},... | collective-permute-start | bytes 49160 | tf_op jit(solution)/shard_map/ppermute | solution.py:225
  5.4 1.7 %collective-permute-done = s32[1,16,256]{2,1,0:T(8,128)S(1)} collective-permute-done((s32[1,16,256]{2,1,0:T(8,128)S(1)}, s32[1,16,256]{2,1,0:T(8,128)S(1)}, u32[]{:S(2)}, u32[]{:S(2)}) %collective-permute-start) | collective-permute-done | bytes 16416 | tf_op jit(solution)/shard_map/ppermute | solution.py:225
  7.2 1.9 %collective-permute-start.1 = (s32[2,16,256]{2,1,0:T(8,128)S(1)}, s32[2,16,256]{2,1,0:T(8,128)S(1)}, u32[]{:S(2)}, u32[]{:S(2)}) collective-permute-start(s32[2,16,256]{2,1,0:T(8,128)S(1)} %pad_add_fusion.2), channel_id=1, source_target_pairs={{0,4},{1,5},{2,6},{3,7},{4,0},{5,1},{6,2},{7,3},{8,12},{9,13},{10,... | collective-permute-start | bytes 98312 | tf_op jit(solution)/shard_map/ppermute | solution.py:225
  9.1 4.3 %tables.1 = (bf16[2,1280,128]{2,1,0:T(8,128)(2,1)}, bf16[1024,128]{1,0:T(8,128)(2,1)}, f32[1024,128]{1,0:T(8,128)}) custom-call(bf16[16,1024]{1,0:T(8,128)(2,1)} %emb_ref.1, f32[1,1024]{1,0:T(1,128)} %bitcast.5, bf16[1024,2304]{1,0:T(8,128)(2,1)} %in_ref.1, f32[2,4,1280]{2,1,0:T(4,128)} %cw_ref.1, f32[2,1280]{1,0:T(2,128)} %cb_ref.1, f32[2,1024]{1,0:T(2,128)} %hg_ref.1), custom_call_target="tpu_custom_call" | custom-call | flops 80000000 | bytes 6000000 | tf_op jit(solution)/shard_map/tables/pallas_call | solution.py:208
  13.4 0.0 collective-permute-done.1
  13.4 1.6 %collective-permute-start.2 = (s32[4,16,256]{2,1,0:T(8,128)S(1)}, s32[4,16,256]{2,1,0:T(8,128)S(1)}, u32[]{:S(2)}, u32[]{:S(2)}) collective-permute-start(s32[4,16,256]{2,1,0:T(8,128)S(1)} %pad_add_fusion.1), channel_id=1, source_target_pairs={{0,2},{1,3},{2,0},{3,1},{4,6},{5,7},{6,4},{7,5},{8,10},{9,11},{10,... | collective-permute-start | bytes 196616 | tf_op jit(solution)/shard_map/ppermute | solution.py:225
  15.0 2.8 %collective-permute-done.2 = s32[4,16,256]{2,1,0:T(8,128)S(1)} collective-permute-done((s32[4,16,256]{2,1,0:T(8,128)S(1)}, s32[4,16,256]{2,1,0:T(8,128)S(1)}, u32[]{:S(2)}, u32[]{:S(2)}) %collective-permute-start.2) | collective-permute-done | bytes 65568 | tf_op jit(solution)/shard_map/ppermute | solution.py:225
  17.8 0.1 collective-permute-start.3
  17.9 1.3 %collective-permute-done.3 = s32[8,16,256]{2,1,0:T(8,128)S(1)} collective-permute-done((s32[8,16,256]{2,1,0:T(8,128)S(1)}, s32[8,16,256]{2,1,0:T(8,128)S(1)}, u32[]{:S(2)}, u32[]{:S(2)}) %collective-permute-start.3) | collective-permute-done | bytes 131104 | tf_op jit(solution)/shard_map/ppermute | solution.py:225
  19.2 0.0 copy-start
  19.2 0.7 %copy-done = s32[16,16,256]{2,1,0:T(8,128)} copy-done((s32[16,16,256]{2,1,0:T(8,128)}, s32[16,16,256]{2,1,0:T(8,128)S(1)}, u32[]{:S(2)}) %copy-start) | copy-done | bytes 262168
  19.9 15.2 %mixer.1 = bf16[256,1024]{1,0:T(8,128)(2,1)} custom-call(s32[1]{0:T(128)} %bitcast.me_ref, f32[2,16]{1,0:T(2,128)} %rates_ref.1, s32[16,16,256]{2,1,0:T(8,128)} %copy-done, bf16[2,1280,128]{2,1,0:T(8,128)(2,1)} %get-tuple-element.8.conv_ref, bf16[1024,128]{1,0:T(8,128)(2,1)} %get-tuple-element.9.gate_ref, f32[1024,128]{1,0:T(8,128)} %get-tuple-element.10.hgt_ref, ...), custom_call_target="tpu_custom_call" | custom-call | flops 12000000000 | bytes 6000000 | tf_op jit(solution)/shard_map/mixer/pallas_call | solution.py:228
  (7 shorter events, 0.0 us)
Async XLA Ops:
  1.4 5.8 %collective-permute-start = (s32[1,16,256]{2,1,0:T(8,128)S(1)}, s32[1,16,256]{2,1,0:T(8,128)S(1)}, u32[]{:S(2)}, u32[]{:S(2)}) collective-permute-start(s32[1,16,256]{2,1,0:T(8,128)S(1)} %get-tuple-element.12), channel_id=1, source_target_pairs={{0,8},{1,9},{2,10},{3,11},{4,12},{5,13},{6,14},{7,15},{8,0},{9,1},... | collective-permute-start | bytes 49160 | tf_op jit(solution)/shard_map/ppermute | solution.py:225
  7.2 6.3 %collective-permute-start.1 = (s32[2,16,256]{2,1,0:T(8,128)S(1)}, s32[2,16,256]{2,1,0:T(8,128)S(1)}, u32[]{:S(2)}, u32[]{:S(2)}) collective-permute-start(s32[2,16,256]{2,1,0:T(8,128)S(1)} %pad_add_fusion.2), channel_id=1, source_target_pairs={{0,4},{1,5},{2,6},{3,7},{4,0},{5,1},{6,2},{7,3},{8,12},{9,13},{10,... | collective-permute-start | bytes 98312 | tf_op jit(solution)/shard_map/ppermute | solution.py:225
  13.4 4.3 %collective-permute-start.2 = (s32[4,16,256]{2,1,0:T(8,128)S(1)}, s32[4,16,256]{2,1,0:T(8,128)S(1)}, u32[]{:S(2)}, u32[]{:S(2)}) collective-permute-start(s32[4,16,256]{2,1,0:T(8,128)S(1)} %pad_add_fusion.1), channel_id=1, source_target_pairs={{0,2},{1,3},{2,0},{3,1},{4,6},{5,7},{6,4},{7,5},{8,10},{9,11},{10,... | collective-permute-start | bytes 196616 | tf_op jit(solution)/shard_map/ppermute | solution.py:225
  17.8 1.4 %collective-permute-start.3 = (s32[8,16,256]{2,1,0:T(8,128)S(1)}, s32[8,16,256]{2,1,0:T(8,128)S(1)}, u32[]{:S(2)}, u32[]{:S(2)}) collective-permute-start(s32[8,16,256]{2,1,0:T(8,128)S(1)} %pad_add_fusion), channel_id=1, source_target_pairs={{0,1},{1,0},{2,3},{3,2},{4,5},{5,4},{6,7},{7,6},{8,9},{9,8},{10,11... | collective-permute-start | bytes 393224 | tf_op jit(solution)/shard_map/ppermute | solution.py:225
  19.2 0.7 %copy-start = (s32[16,16,256]{2,1,0:T(8,128)}, s32[16,16,256]{2,1,0:T(8,128)S(1)}, u32[]{:S(2)}) copy-start(s32[16,16,256]{2,1,0:T(8,128)S(1)} %constant_dynamic-update-slice_fusion.data_ref) | copy-start | bytes 786436
where the time goes:
time: 35.4 us; the launch traced here: 35.1 us
  Pallas kernels  19.6 us (55%)
  starting transfers between devices  7.57 us (21%)
  waiting for transfers between devices  5.8 us (16%)
  other arithmetic  1.42 us (4%)
  local copies, waits for them, and re-layouts  0.74 us (2%)
    pallas_call x1, Pallas kernels, shards(): pl.pallas_call(functools.partial(mixer_kernel, count, bits), out_shape=ja...  15.2 us
    ppermute x4, starting transfers between devices, shards(): other = lax.ppermute(held, 'seq', [(i, i ^ far) for i in range(count)])  7.57 us
    ppermute x4, waiting for transfers between devices, shards(): other = lax.ppermute(held, 'seq', [(i, i ^ far) for i in range(count)])  5.8 us
    pallas_call x1, Pallas kernels, shards(): pl.pallas_call(tables_kernel, out_shape=(jax.ShapeDtypeStruct((2, wide, 2...  4.35 us
    unnamed x5, local copies, waits for them, and re-layouts  0.73 us
    unnamed x1, other arithmetic  0.72 us
  transfers between devices with their start and end apart: 4, of which 3 were waited for; matrix products, arithmetic and copies ran while one was open for 0% of the time, Pallas kernels for 12%

commit v1 on v0

v1 whole, which is shorter than its diff:
```python
import functools

import jax
import jax.numpy as jnp
from jax import lax
from jax.experimental import pallas as pl
from jax.experimental.pallas import tpu as pltpu
from jax.sharding import PartitionSpec as P

EPS = 1e-05
LOG2E = 1.4426950408889634
F32 = jnp.float32
BF16 = jnp.bfloat16
NT = (((1,), (1,)), ((), ()))
TN = (((0,), (0,)), ((), ()))
MIB = 1024 * 1024
LANES = 128


def dot(a, b, dims=(((1,), (0,)), ((), ()))):
    return lax.dot_general(a, b, dims, preferred_element_type=F32)


def split(value):
    high = value.astype(BF16)
    return high, (value - high.astype(F32)).astype(BF16)


def sums_before(e):
    span = e.shape[1]
    lower = lax.broadcasted_iota(jnp.int32, (span, span), 0)
    upper = lax.broadcasted_iota(jnp.int32, (span, span), 1)
    before = jnp.where(lower < upper, 1.0, 0.0).astype(BF16)
    high = dot((e >> 8).astype(F32).astype(BF16), before)
    low = dot((e & 255).astype(F32).astype(BF16), before)
    return 256.0 * high + low


def pack_kernel(ids_ref, exp_ref, out_ref, ids_buf, exp_buf, sems):
    a = pltpu.make_async_copy(ids_ref, ids_buf, sems.at[0])
    b = pltpu.make_async_copy(exp_ref, exp_buf, sems.at[1])
    a.start()
    b.start()
    a.wait()
    b.wait()
    out_ref[0] = (exp_buf[...] - 1) + (ids_buf[...] << 16)


def prep_kernel(
    exp_hbm, rates_hbm, emb_hbm, gain_hbm, in_hbm, cw_hbm, cb_hbm, hg_hbm,
    conv_ref, gate_ref, hgt_ref, rate_ref, decay_ref,
    exp_ref, rates_ref, emb_ref, gain_ref, in_ref, cw_ref, cb_ref, hg_ref, sems,
):
    vocab = emb_ref.shape[0]
    inner = hg_ref.shape[1]
    taps = cw_ref.shape[1]
    heads, span = exp_ref.shape
    small = [
        pltpu.make_async_copy(src, dst, sems.at[i])
        for i, (src, dst) in enumerate(
            [
                (exp_hbm, exp_ref), (rates_hbm, rates_ref), (emb_hbm, emb_ref),
                (gain_hbm, gain_ref), (cw_hbm, cw_ref), (cb_hbm, cb_ref), (hg_hbm, hg_ref),
            ]
        )
    ]
    gate_copy = pltpu.make_async_copy(
        in_hbm.at[:, pl.ds(0, inner)], in_ref.at[:, pl.ds(0, inner)], sems.at[7]
    )
    conv_copy = pltpu.make_async_copy(
        in_hbm.at[:, pl.ds(inner, in_ref.shape[1] - inner)],
        in_ref.at[:, pl.ds(inner, in_ref.shape[1] - inner)],
        sems.at[8],
    )
    for copy in small:
        copy.start()
    gate_copy.start()
    conv_copy.start()
    for copy in small:
        copy.wait()

    e = exp_ref[...]
    pre = sums_before(e)
    inc = pre + e.astype(F32)
    rates = jnp.concatenate([rates_ref[...], jnp.zeros((6, heads), F32)], axis=0).T
    half = span // 2
    lower = lax.broadcasted_iota(jnp.int32, (half, half), 0)
    upper = lax.broadcasted_iota(jnp.int32, (half, half), 1)
    zero = jnp.zeros((half, half), BF16)
    for b in range(2):
        rate_ref[b] = jnp.broadcast_to(rates[:, b : b + 1], (heads, span))
        cum = inc if b == 0 else pre
        cum_col = cum.T
        keep = lower <= upper if b == 0 else lower >= upper
        factor = rate_ref[b] * (-LOG2E if b == 0 else LOG2E)
        for h in range(heads):
            for p in range(2):
                for q in range(2):
                    rows = slice(p * half, (p + 1) * half)
                    cols = slice(q * half, (q + 1) * half)
                    if (p > q) if b == 0 else (p < q):
                        decay_ref[b, h, rows, cols] = zero
                        continue
                    gap = cum[h : h + 1, cols] - cum_col[rows, h : h + 1]
                    value = jnp.exp2(gap * factor[h : h + 1, :half])
                    if p == q:
                        value = jnp.where(keep, value, 0.0)
                    decay_ref[b, h, rows, cols] = value.astype(BF16)
    hg = jnp.concatenate([hg_ref[...], jnp.zeros((LANES - 2, inner), F32)], axis=0)
    hgt_ref[...] = hg.T

    em = emb_ref[...].astype(F32)
    norm = em * lax.rsqrt(jnp.mean(em * em, axis=1, keepdims=True) + EPS) * gain_ref[...]
    norm = norm.astype(BF16)
    gate_copy.wait()
    gate = dot(norm, in_ref[:, :inner]).astype(BF16).astype(F32)
    gate = gate / (1.0 + jnp.exp(-gate))
    g0 = gate.astype(BF16)
    g1, g2 = split(gate - g0.astype(F32))
    pad = jnp.zeros((gate_ref.shape[1] - 3 * vocab, inner), BF16)
    gate_ref[...] = jnp.concatenate([g0, g1, g2, pad], axis=0).T
    conv_copy.wait()
    proj = dot(norm, in_ref[:, inner:]).astype(BF16).astype(F32)
    for b in range(2):
        rows = []
        for j in range(taps):
            row = cw_ref[b, j : j + 1, :] * proj
            if j == taps - 1:
                row = row + cb_ref[b : b + 1, :]
            rows.append(0.5 * row)
        high, low = split(jnp.concatenate(rows, axis=0))
        conv_ref[b] = jnp.concatenate([high, low], axis=0).T


def mixer_kernel(
    masks,
    near_ref, far_ref, conv_ref, gate_ref, hgt_ref, rate_ref, decay_ref, out_proj_ref,
    mixed_hbm,
    expo, within, total, ids, shifted, x_held, b_held, state, mixin, mixed, sems,
):
    count = len(masks)
    heads, span = near_ref.shape[1], near_ref.shape[2]
    inner = out_proj_ref.shape[0]
    head = inner // heads
    width = (conv_ref.shape[1] - inner) // 2
    vocab = conv_ref.shape[2] // 8
    me = lax.axis_index("seq")

    for slot, mask in enumerate(masks):
        c = jnp.bitwise_xor(me, mask)
        raw = near_ref[slot] if slot < count // 2 else far_ref[slot - count // 2]
        expo[c] = (raw & 0xFFFF) + 1
        ids[pl.ds(c, 1), :] = raw[0:1] >> 16

    e = expo[...].reshape(count * heads, span)
    pre = sums_before(e)
    within[0] = pre.reshape(count, heads, span)
    inc = pre + e.astype(F32)
    tot = jnp.broadcast_to(inc[:, span - 1 :], inc.shape)
    total[...] = tot.reshape(count, heads, span)
    within[1] = (tot - inc).reshape(count, heads, span)

    tok = ids[...]
    lane = lax.broadcasted_iota(jnp.int32, tok.shape, 1)
    row = lax.broadcasted_iota(jnp.int32, tok.shape, 0)
    for d in range(-3, 4):
        if d == 0:
            moved = tok
        elif d < 0:
            here = pltpu.roll(tok, -d, axis=1)
            other = jnp.where(row == 0, -1, pltpu.roll(here, 1, axis=0))
            moved = jnp.where(lane < -d, other, here)
        else:
            here = pltpu.roll(tok, span - d, axis=1)
            other = jnp.where(row == count - 1, -1, pltpu.roll(here, count - 1, axis=0))
            moved = jnp.where(lane >= span - d, other, here)
        shifted[d + 3] = moved

    values = lax.broadcasted_iota(jnp.int32, (vocab, span), 0)

    def onehot(c, sign):
        rows = []
        for j in range(4):
            token = shifted[3 + (j - 3) * sign, pl.ds(c, 1), :]
            rows.append(jnp.where(values == token, 1.0, 0.0))
        one = jnp.concatenate(rows, axis=0).astype(BF16)
        return jnp.concatenate([one, one], axis=0)

    def convolve(table, one):
        half = dot(table, one)
        return half + half * jnp.tanh(half)

    def remote(i, slot, run):
        rev = i >= me
        b = rev.astype(jnp.int32)
        c = jnp.clip(jnp.where(rev, i + 1, me - 1 - i), 0, count - 1)
        run = jnp.where(i == me, 0.0, run)
        decay = jnp.exp(-rate_ref[b] * (within[1 - b, c] + run))
        one = onehot(c, 1 - 2 * b)
        x = convolve(conv_ref[b, :inner, :], one)
        x = x.reshape(heads, head, span) * decay[:, None, :]
        x_held[slot] = x.reshape(inner, span).astype(BF16)
        bt = convolve(conv_ref[b, inner : inner + width, :], one)
        ahead = jnp.where(rev, 0.0, bt)
        behind = jnp.where(jnp.logical_and(rev, i < count - 1), bt, 0.0)
        b_held[slot] = jnp.concatenate([ahead, behind], axis=0).astype(BF16)
        return run + total[c]

    group = x_held.shape[0]

    def gather(g, run, first):
        for k in range(group):
            run = remote(g * group + k, k, run)
        for r in range(0, inner, 512):
            part = jnp.zeros((512, 2 * width), F32)
            for k in range(group):
                part = part + dot(x_held[k, r : r + 512], b_held[k], NT)
            state[r : r + 512] = part if first else state[r : r + 512] + part
        return run

    run = gather(0, jnp.zeros((heads, span), F32), True)
    if count - 1 > group:
        lax.fori_loop(1, pl.cdiv(count - 1, group), lambda g, run: gather(g, run, False), run)

    own_pre = within[0, me]
    own_inc = own_pre + expo[me].astype(F32)
    own_rest = total[me] - own_pre
    current = jnp.where(values == ids[pl.ds(me, 1), :], 1.0, 0.0).astype(BF16)
    current = jnp.concatenate(
        [current] * 3 + [jnp.zeros((gate_ref.shape[1] - 3 * vocab, span), BF16)], axis=0
    )
    gates = dot(gate_ref[...], current)
    for b in range(2):
        one = onehot(me, 1 - 2 * b)
        conv = convolve(conv_ref[b], one).astype(BF16)
        xt = conv[:inner]
        bt = conv[inner : inner + width]
        ct = conv[inner + width :]
        scores = dot(bt, ct, TN).astype(BF16)
        reach = jnp.exp(-rate_ref[b] * (own_inc if b == 0 else own_rest))
        high, low = split(state[:, b * width : (b + 1) * width])
        carried = dot(
            jnp.concatenate([high, low], axis=1), jnp.concatenate([ct, ct], axis=0)
        )
        for h in range(heads):
            rows = slice(h * head, (h + 1) * head)
            y = dot(xt[rows], scores * decay_ref[b, h])
            y = y + reach[h : h + 1] * carried[rows]
            v = y * gates[rows]
            inv = lax.rsqrt(jnp.sum(v * v, axis=0, keepdims=True) * (1.0 / head) + EPS)
            out = v * inv * hgt_ref[rows, b : b + 1]
            if b == 0:
                mixin[rows] = out
            else:
                mixin[rows] = mixin[rows] + out
    both = mixin[...].astype(BF16).T
    width_out = mixed.shape[1] // 4
    copies = []
    for k in range(4):
        cols = pl.ds(k * width_out, width_out)
        mixed[:, cols] = dot(both, out_proj_ref[:, cols]).astype(BF16)
        copies.append(pltpu.make_async_copy(mixed.at[:, cols], mixed_hbm.at[:, cols], sems.at[k]))
        copies[-1].start()
    for copy in copies:
        copy.wait()


def shards(
    ids, exponents, embedding, norm_gain, in_proj, conv_weight, conv_bias, rates, head_gain, out_proj
):
    count = lax.axis_size("seq")
    bits = count.bit_length() - 1
    heads, span = exponents.shape
    vocab = embedding.shape[0]
    inner = out_proj.shape[0]
    wide = conv_bias.shape[1]
    width = (wide - inner) // 2
    taps = conv_weight.shape[1]
    group = min(count - 1, 16)
    pin = lambda value: pltpu.with_memory_space_constraint(value, pltpu.HBM)
    vmem = pl.BlockSpec(memory_space=pltpu.VMEM)
    hbm = pl.BlockSpec(memory_space=pltpu.HBM)
    f32 = lambda *shape: jax.ShapeDtypeStruct(shape, F32)
    b16 = lambda *shape: jax.ShapeDtypeStruct(shape, BF16)

    packed = pl.pallas_call(
        pack_kernel,
        out_shape=jax.ShapeDtypeStruct((1, heads, span), jnp.int32),
        in_specs=[hbm, hbm],
        out_specs=vmem,
        scratch_shapes=[
            pltpu.VMEM((1, span), jnp.int32),
            pltpu.VMEM((heads, span), jnp.int32),
            pltpu.SemaphoreType.DMA((2,)),
        ],
        compiler_params=pltpu.CompilerParams(vmem_limit_bytes=MIB),
        name="pack",
    )(pin(ids[None, :]), pin(exponents))

    def swap(value, mask):
        return lax.ppermute(value, "seq", [(i, i ^ mask) for i in range(count)])

    stages = [[count // 2, count // 2 + count // 4, count // 4]]
    stages += [[1 << bit] for bit in reversed(range(bits - 2))]
    tables = pl.pallas_call(
        prep_kernel,
        out_shape=(
            b16(2, wide, 2 * taps * vocab),
            b16(inner, LANES),
            f32(inner, LANES),
            f32(2, heads, span),
            b16(2, heads, span, span),
        ),
        in_specs=[hbm] * 8,
        out_specs=(vmem,) * 5,
        scratch_shapes=[
            pltpu.VMEM((heads, span), jnp.int32),
            pltpu.VMEM((2, heads), F32),
            pltpu.VMEM(embedding.shape, BF16),
            pltpu.VMEM((1, inner), F32),
            pltpu.VMEM(in_proj.shape, BF16),
            pltpu.VMEM(conv_weight.shape, F32),
            pltpu.VMEM(conv_bias.shape, F32),
            pltpu.VMEM(head_gain.shape, F32),
            pltpu.SemaphoreType.DMA((9,)),
        ],
        compiler_params=pltpu.CompilerParams(vmem_limit_bytes=16 * MIB),
        name="prep",
        cost_estimate=pl.CostEstimate(
            flops=100_000_000, bytes_accessed=12_000_000, transcendentals=2_000_000
        ),
    )(*map(pin, (exponents, rates, embedding, norm_gain[None, :], in_proj, conv_weight, conv_bias, head_gain)))

    held, masks = packed, [0]
    for k, stage in enumerate(stages[:-1]):
        held = jnp.concatenate([held] + [swap(held, mask) for mask in stage], axis=0)
        masks = masks + [m ^ mask for mask in stage for m in masks]
        if k == 0:
            held, tables = lax.optimization_barrier((held, tables))
    far = swap(held, 1)
    masks = masks + [m ^ 1 for m in masks]

    return pl.pallas_call(
        functools.partial(mixer_kernel, masks),
        out_shape=b16(span, inner),
        in_specs=[vmem] * 8,
        out_specs=hbm,
        scratch_shapes=[
            pltpu.VMEM((count, heads, span), jnp.int32),
            pltpu.VMEM((2, count, heads, span), F32),
            pltpu.VMEM((count, heads, span), F32),
            pltpu.VMEM((count, span), jnp.int32),
            pltpu.VMEM((7, count, span), jnp.int32),
            pltpu.VMEM((group, inner, span), BF16),
            pltpu.VMEM((group, 2 * width, span), BF16),
            pltpu.VMEM((inner, 2 * width), F32),
            pltpu.VMEM((inner, span), F32),
            pltpu.VMEM((span, inner), BF16),
            pltpu.SemaphoreType.DMA((4,)),
        ],
        compiler_params=pltpu.CompilerParams(vmem_limit_bytes=(24 if count <= 32 else 40) * MIB),
        name="mixer",
        cost_estimate=pl.CostEstimate(
            flops=20_000_000_000, bytes_accessed=6_000_000, transcendentals=6_000_000
        ),
    )(held, far, *tables, out_proj)


def solution(mesh):
    in_specs = (
        P(("parts", "seq")),
        P(None, ("parts", "seq")),
        P(), P(), P(), P(), P(), P(), P(), P(),
    )
    out_specs = P(("parts", "seq"), None)
    return jax.shard_map(shards, mesh=mesh, in_specs=in_specs, out_specs=out_specs, check_vma=False)
```

time: 35.4 us -> 25.5 us (0.72)
  Pallas kernels: 19.6 us -> 13.2 us
  other arithmetic: 1.42 us -> 0.01 us
  waiting for transfers between devices: 5.8 us -> 4.75 us
  local copies, waits for them, and re-layouts: 0.74 us -> 0.01 us
  starting transfers between devices: 7.57 us -> 7.17 us
    pallas_call x2 -> x3, Pallas kernels: 19.6 us -> 13.2 us  [the longest x1 8.42 us: shards(): pl.pallas_call(functools.partial(mixer_kernel, masks), out_shape=b16(span...]
    ppermute x4 -> x5, waiting for transfers between devices: 5.8 us -> 4.75 us  [swap(): return lax.ppermute(value, 'seq', [(i, i ^ mask) for i in range(count)])]
    unnamed x1 -> x0, other arithmetic: 0.72 us -> none
    unnamed x5 -> x3, local copies, waits for them, and re-layouts: 0.73 us -> 0.01 us
    shift_left x1 -> x0, other arithmetic: 0.68 us -> none  [shards(): held = (exponents - 1 + (ids << 16)[None, :])[None]]
    ppermute x4 -> x5, starting transfers between devices: 7.57 us -> 7.17 us  [swap(): return lax.ppermute(value, 'seq', [(i, i ^ mask) for i in range(count)])]
  transfers between devices with their start and end apart: 4 -> 5, of which waited for: 3 -> 3; matrix products, arithmetic and copies ran while one was open for 0% -> 0% of each run, Pallas kernels for 12% -> 15%
where the time goes in v1:
time: 25.5 us; the launch traced here: 25.2 us
  Pallas kernels  13.2 us (52%)
  starting transfers between devices  7.17 us (28%)
  waiting for transfers between devices  4.75 us (19%)
    pallas_call x1, Pallas kernels, shards(): pl.pallas_call(functools.partial(mixer_kernel, masks), out_shape=b16(span...  8.42 us
    ppermute x5, starting transfers between devices, swap(): return lax.ppermute(value, 'seq', [(i, i ^ mask) for i in range(count)])  7.17 us
    ppermute x5, waiting for transfers between devices, swap(): return lax.ppermute(value, 'seq', [(i, i ^ mask) for i in range(count)])  4.75 us
    pallas_call x1, Pallas kernels, shards(): pl.pallas_call(prep_kernel, out_shape=(b16(2, wide, 2 * taps * vocab), b1...  3.86 us
    pallas_call x1, Pallas kernels, shards(): pl.pallas_call(pack_kernel, out_shape=jax.ShapeDtypeStruct((1, heads, spa...  0.9 us
  transfers between devices with their start and end apart: 5, of which 3 were waited for; matrix products, arithmetic and copies ran while one was open for 0% of the time, Pallas kernels for 15%

profile of v1, /device:TPU:0, one launch (start us, length us, event | category | flops | bytes accessed | tf_op | source)
XLA Modules:
  0.0 25.2 jit_solution(7827235718842041385)
XLA Ops:
  0.0 0.0 copy-start
  0.0 0.9 %pack.1 = s32[1,16,256]{2,1,0:T(8,128)S(1)} custom-call(s32[1,256]{1,0:T(1,128)} %bitcast.3, s32[16,256]{1,0:T(8,128)} %exp_hbm.1), custom_call_target="tpu_custom_call" | custom-call | tf_op jit(solution)/shard_map/pack/pallas_call | solution.py:286
  0.9 3.1 %collective-permute-start.2 = (s32[1,16,256]{2,1,0:T(8,128)S(1)}, s32[1,16,256]{2,1,0:T(8,128)S(1)}, u32[]{:S(2)}, u32[]{:S(2)}) collective-permute-start(s32[1,16,256]{2,1,0:T(8,128)S(1)} %pack.1), channel_id=1, source_target_pairs={{0,4},{1,5},{2,6},{3,7},{4,0},{5,1},{6,2},{7,3},{8,12},{9,13},{10,... | collective-permute-start | bytes 49160 | tf_op jit(solution)/shard_map/ppermute | solution.py:301
  4.0 2.5 %collective-permute-start.1 = (s32[1,16,256]{2,1,0:T(8,128)S(1)}, s32[1,16,256]{2,1,0:T(8,128)S(1)}, u32[]{:S(2)}, u32[]{:S(2)}) collective-permute-start(s32[1,16,256]{2,1,0:T(8,128)S(1)} %pack.1), channel_id=1, source_target_pairs={{0,12},{1,13},{2,14},{3,15},{4,8},{5,9},{6,10},{7,11},{8,4},{9,5},... | collective-permute-start | bytes 49160 | tf_op jit(solution)/shard_map/ppermute | solution.py:301
  6.5 0.1 collective-permute-start
  6.6 3.9 %prep.1 = (bf16[2,1280,128]{2,1,0:T(8,128)(2,1)S(1)}, bf16[1024,128]{1,0:T(8,128)(2,1)S(1)}, f32[1024,128]{1,0:T(8,128)S(1)}, f32[2,16,256]{2,1,0:T(8,128)S(1)}, bf16[2,16,256,256]{3,2,1,0:T(8,128)(2,1)S(1)}) custom-call(s32[16,256]{1,0:T(8,128)} %exp_hbm.1, f32[2,16]{1,0:T(2,128)} %rates_hbm.1, bf16[16,1024]{1,0:T(8,128)(2,1)} %emb_hbm.1, ...), custom_call_target="tpu_custom_call" | custom-call | flops 100000000 | bytes 12000000 | tf_op jit(solution)/shard_map/prep/pallas_call | solution.py:305
  10.5 0.0 collective-permute-done.2
  10.5 0.0 collective-permute-done.1
  10.5 0.6 %collective-permute-done = s32[1,16,256]{2,1,0:T(8,128)S(1)} collective-permute-done((s32[1,16,256]{2,1,0:T(8,128)S(1)}, s32[1,16,256]{2,1,0:T(8,128)S(1)}, u32[]{:S(2)}, u32[]{:S(2)}) %collective-permute-start) | collective-permute-done | bytes 16416 | tf_op jit(solution)/shard_map/ppermute | solution.py:301
  11.1 1.5 %collective-permute-start.3 = (s32[4,16,256]{2,1,0:T(8,128)S(1)}, s32[4,16,256]{2,1,0:T(8,128)S(1)}, u32[]{:S(2)}, u32[]{:S(2)}) collective-permute-start(s32[4,16,256]{2,1,0:T(8,128)S(1)} %pad_add_fusion), channel_id=1, source_target_pairs={{0,2},{1,3},{2,0},{3,1},{4,6},{5,7},{6,4},{7,5},{8,10},{9,11},{10,... | collective-permute-start | bytes 196616 | tf_op jit(solution)/shard_map/ppermute | solution.py:301
  12.6 2.8 %collective-permute-done.3 = s32[4,16,256]{2,1,0:T(8,128)S(1)} collective-permute-done((s32[4,16,256]{2,1,0:T(8,128)S(1)}, s32[4,16,256]{2,1,0:T(8,128)S(1)}, u32[]{:S(2)}, u32[]{:S(2)}) %collective-permute-start.3) | collective-permute-done | bytes 65568 | tf_op jit(solution)/shard_map/ppermute | solution.py:301
  15.4 0.0 collective-permute-start.4
  15.4 1.3 %collective-permute-done.4.far_ref = s32[8,16,256]{2,1,0:T(8,128)S(1)} collective-permute-done((s32[8,16,256]{2,1,0:T(8,128)S(1)}, s32[8,16,256]{2,1,0:T(8,128)S(1)}, u32[]{:S(2)}, u32[]{:S(2)}) %collective-permute-start.4) | collective-permute-done | bytes 131104 | tf_op jit(solution)/shard_map/ppermute | solution.py:301
  16.8 0.0 copy-done
  16.8 8.4 %mixer.1 = bf16[256,1024]{1,0:T(8,128)(2,1)} custom-call(s32[8,16,256]{2,1,0:T(8,128)S(1)} %constant_dynamic-update-slice_fusion.near_ref, s32[8,16,256]{2,1,0:T(8,128)S(1)} %collective-permute-done.4.far_ref, bf16[2,1280,128]{2,1,0:T(8,128)(2,1)S(1)} %get-tuple-element.22.conv_ref, bf16[1024,128]{1,0:T(8,128)(2,1)S(1)} %get-tuple-element.23.gate_ref, ...), custom_call_target="tpu_custom_call" | custom-call | flops 20000000000 | bytes 6000000 | tf_op jit(solution)/shard_map/mixer/pallas_call | solution.py:343
  (3 shorter events, 0.0 us)
Async XLA Ops:
  0.0 16.8 %copy-start = (bf16[1024,1024]{1,0:T(8,128)(2,1)S(1)}, bf16[1024,1024]{1,0:T(8,128)(2,1)}, u32[]{:S(2)}) copy-start(bf16[1024,1024]{1,0:T(8,128)(2,1)} %out_proj_ref.1) | copy-start | bytes 6291460
  0.9 9.6 %collective-permute-start.2 = (s32[1,16,256]{2,1,0:T(8,128)S(1)}, s32[1,16,256]{2,1,0:T(8,128)S(1)}, u32[]{:S(2)}, u32[]{:S(2)}) collective-permute-start(s32[1,16,256]{2,1,0:T(8,128)S(1)} %pack.1), channel_id=1, source_target_pairs={{0,4},{1,5},{2,6},{3,7},{4,0},{5,1},{6,2},{7,3},{8,12},{9,13},{10,... | collective-permute-start | bytes 49160 | tf_op jit(solution)/shard_map/ppermute | solution.py:301
  4.0 6.5 %collective-permute-start.1 = (s32[1,16,256]{2,1,0:T(8,128)S(1)}, s32[1,16,256]{2,1,0:T(8,128)S(1)}, u32[]{:S(2)}, u32[]{:S(2)}) collective-permute-start(s32[1,16,256]{2,1,0:T(8,128)S(1)} %pack.1), channel_id=1, source_target_pairs={{0,12},{1,13},{2,14},{3,15},{4,8},{5,9},{6,10},{7,11},{8,4},{9,5},... | collective-permute-start | bytes 49160 | tf_op jit(solution)/shard_map/ppermute | solution.py:301
  6.5 4.6 %collective-permute-start = (s32[1,16,256]{2,1,0:T(8,128)S(1)}, s32[1,16,256]{2,1,0:T(8,128)S(1)}, u32[]{:S(2)}, u32[]{:S(2)}) collective-permute-start(s32[1,16,256]{2,1,0:T(8,128)S(1)} %pack.1), channel_id=1, source_target_pairs={{0,8},{1,9},{2,10},{3,11},{4,12},{5,13},{6,14},{7,15},{8,0},{9,1},... | collective-permute-start | bytes 49160 | tf_op jit(solution)/shard_map/ppermute | solution.py:301
  11.1 4.3 %collective-permute-start.3 = (s32[4,16,256]{2,1,0:T(8,128)S(1)}, s32[4,16,256]{2,1,0:T(8,128)S(1)}, u32[]{:S(2)}, u32[]{:S(2)}) collective-permute-start(s32[4,16,256]{2,1,0:T(8,128)S(1)} %pad_add_fusion), channel_id=1, source_target_pairs={{0,2},{1,3},{2,0},{3,1},{4,6},{5,7},{6,4},{7,5},{8,10},{9,11},{10,... | collective-permute-start | bytes 196616 | tf_op jit(solution)/shard_map/ppermute | solution.py:301
  15.4 1.3 %collective-permute-start.4 = (s32[8,16,256]{2,1,0:T(8,128)S(1)}, s32[8,16,256]{2,1,0:T(8,128)S(1)}, u32[]{:S(2)}, u32[]{:S(2)}) collective-permute-start(s32[8,16,256]{2,1,0:T(8,128)S(1)} %constant_dynamic-update-slice_fusion.near_ref), channel_id=1, source_target_pairs={{0,1},{1,0},{2,3},{3,2},{4,5},{5,4},{6,7},{7,6},{8,9},{9,8},{10,11... | collective-permute-start | bytes 393224 | tf_op jit(solution)/shard_map/ppermute | solution.py:301

commit v2 on v1

v2 whole, which is shorter than its diff:
```python
import functools

import jax
import jax.numpy as jnp
from jax import lax
from jax.experimental import pallas as pl
from jax.experimental.pallas import tpu as pltpu
from jax.sharding import PartitionSpec as P

EPS = 1e-05
LOG2E = 1.4426950408889634
F32 = jnp.float32
BF16 = jnp.bfloat16
NT = (((1,), (1,)), ((), ()))
TN = (((0,), (0,)), ((), ()))
MIB = 1024 * 1024
LANES = 128


def dot(a, b, dims=(((1,), (0,)), ((), ()))):
    return lax.dot_general(a, b, dims, preferred_element_type=F32)


def split(value):
    high = value.astype(BF16)
    return high, (value - high.astype(F32)).astype(BF16)


def sums_before(e):
    span = e.shape[1]
    lower = lax.broadcasted_iota(jnp.int32, (span, span), 0)
    upper = lax.broadcasted_iota(jnp.int32, (span, span), 1)
    before = jnp.where(lower < upper, 1.0, 0.0).astype(BF16)
    high = dot((e >> 8).astype(F32).astype(BF16), before)
    low = dot((e & 255).astype(F32).astype(BF16), before)
    return 256.0 * high + low


def convolve(table, one):
    half = dot(table, one)
    return half + half * jnp.tanh(half)


def pack_kernel(ids_ref, exp_ref, out_ref, ids_buf, exp_buf, sems):
    a = pltpu.make_async_copy(ids_ref, ids_buf, sems.at[0])
    b = pltpu.make_async_copy(exp_ref, exp_buf, sems.at[1])
    a.start()
    b.start()
    a.wait()
    b.wait()
    out_ref[0] = (exp_buf[...] - 1) + (ids_buf[...] << 16)


def prep_kernel(
    rates_hbm, emb_hbm, gain_hbm, in_hbm, cw_hbm, cb_hbm, hg_hbm,
    conv_ref, norm_ref, hgt_ref, rate_ref,
    rates_ref, emb_ref, gain_ref, in_ref, cw_ref, cb_ref, hg_ref, sems,
):
    inner = hg_ref.shape[1]
    taps = cw_ref.shape[1]
    heads, span = rate_ref.shape[1:]
    small = [
        pltpu.make_async_copy(src, dst, sems.at[i])
        for i, (src, dst) in enumerate(
            [
                (rates_hbm, rates_ref), (emb_hbm, emb_ref), (gain_hbm, gain_ref),
                (cw_hbm, cw_ref), (cb_hbm, cb_ref), (hg_hbm, hg_ref),
            ]
        )
    ]
    block = in_ref.shape[1] // 2
    wanted = [
        pltpu.make_async_copy(
            in_hbm.at[:, pl.ds(inner + k * block, block)], in_ref.at[:, pl.ds(k * block, block)],
            sems.at[len(small) + k],
        )
        for k in range(2)
    ]
    for copy in small + wanted:
        copy.start()
    for copy in small:
        copy.wait()
    rates = jnp.concatenate([rates_ref[...], jnp.zeros((6, heads), F32)], axis=0).T
    for b in range(2):
        rate_ref[b] = jnp.broadcast_to(rates[:, b : b + 1], (heads, span))
    hg = jnp.concatenate([hg_ref[...], jnp.zeros((LANES - 2, inner), F32)], axis=0)
    hgt_ref[...] = hg.T
    em = emb_ref[...].astype(F32)
    norm = em * lax.rsqrt(jnp.mean(em * em, axis=1, keepdims=True) + EPS) * gain_ref[...]
    norm = norm.astype(BF16)
    norm_ref[...] = norm
    for k, copy in enumerate(wanted):
        copy.wait()
        cols = slice(k * block, (k + 1) * block)
        proj = dot(norm, in_ref[:, cols]).astype(BF16).astype(F32)
        for b in range(2):
            rows = []
            for j in range(taps):
                row = cw_ref[b, j : j + 1, cols] * proj
                if j == taps - 1:
                    row = row + cb_ref[b : b + 1, cols]
                rows.append(0.5 * row)
            high, low = split(jnp.concatenate(rows, axis=0))
            conv_ref[b, cols] = jnp.concatenate([high, low], axis=0).T


def local_kernel(
    held_ref, rate_ref, norm_ref, in_hbm, decay_ref, gates_ref, reach_ref, in_ref, sem
):
    inner = gates_ref.shape[0]
    fetch = pltpu.make_async_copy(in_hbm.at[:, pl.ds(0, inner)], in_ref, sem)
    fetch.start()
    heads, span = held_ref.shape[1:]
    e = (held_ref[0] & 0xFFFF) + 1
    pre = sums_before(e)
    inc = pre + e.astype(F32)
    half = span // 2
    lower = lax.broadcasted_iota(jnp.int32, (half, half), 0)
    upper = lax.broadcasted_iota(jnp.int32, (half, half), 1)
    zero = jnp.zeros((half, half), BF16)
    for b in range(2):
        cum = inc if b == 0 else pre
        cum_col = cum.T
        keep = lower <= upper if b == 0 else lower >= upper
        factor = rate_ref[b] * (-LOG2E if b == 0 else LOG2E)
        for h in range(heads):
            for p in range(2):
                for q in range(2):
                    rows = slice(p * half, (p + 1) * half)
                    cols = slice(q * half, (q + 1) * half)
                    if (p > q) if b == 0 else (p < q):
                        decay_ref[b, h, rows, cols] = zero
                        continue
                    gap = cum[h : h + 1, cols] - cum_col[rows, h : h + 1]
                    value = jnp.exp2(gap * factor[h : h + 1, :half])
                    if p == q:
                        value = jnp.where(keep, value, 0.0)
                    decay_ref[b, h, rows, cols] = value.astype(BF16)
    reach_ref[0] = jnp.exp(-rate_ref[0] * inc)
    reach_ref[1] = jnp.exp(-rate_ref[1] * (inc[:, span - 1 :] - pre))
    vocab = norm_ref.shape[0]
    values = lax.broadcasted_iota(jnp.int32, (vocab, span), 0)
    current = jnp.where(values == (held_ref[0, 0:1] >> 16), 1.0, 0.0).astype(BF16)
    current = jnp.concatenate([current] * 3 + [jnp.zeros_like(current)], axis=0)
    fetch.wait()
    gate = dot(norm_ref[...], in_ref[...]).astype(BF16).astype(F32)
    gate = gate / (1.0 + jnp.exp(-gate))
    g0 = gate.astype(BF16)
    g1, g2 = split(gate - g0.astype(F32))
    gate = jnp.concatenate([g0, g1, g2, jnp.zeros_like(g0)], axis=0)
    gates_ref[...] = dot(gate, current, TN)


def unpack(raw):
    e = (raw & 0xFFFF) + 1
    pre = sums_before(e)
    inc = pre + e.astype(F32)
    tot = jnp.broadcast_to(inc[:, inc.shape[1] - 1 :], inc.shape)
    return pre, tot - inc, tot


def turn_kernel(near_ref, out_ref, turned_ref):
    turned_ref[...] = out_ref[...].T


def states_kernel(
    masks,
    near_ref, far_ref, conv_ref, rate_ref,
    mine_ref, mate_ref, onehot_ref,
    within, total, ids, shifted, x_held, b_held, state,
):
    count = len(masks)
    heads, span = near_ref.shape[1:]
    group, rows, _ = x_held.shape
    width = b_held.shape[1] // 2
    inner = conv_ref.shape[1] - 2 * width
    head = inner // heads
    vocab = conv_ref.shape[2] // 8
    me = lax.axis_index("seq")
    core = me & 1
    base = me - core

    for side, ref in enumerate((near_ref, far_ref)):
        pre, post, tot = unpack(ref[...].reshape(count // 2 * heads, span))
        for slot in range(count // 2):
            c = jnp.bitwise_xor(me, masks[side * (count // 2) + slot])
            block = slice(slot * heads, (slot + 1) * heads)
            within[0, c] = pre[block]
            within[1, c] = post[block]
            total[c] = tot[block]
            ids[pl.ds(c, 1), :] = ref[slot, 0:1] >> 16

    tok = ids[...]
    lane = lax.broadcasted_iota(jnp.int32, tok.shape, 1)
    row = lax.broadcasted_iota(jnp.int32, tok.shape, 0)
    for d in range(-3, 4):
        if d == 0:
            moved = tok
        elif d < 0:
            here = pltpu.roll(tok, -d, axis=1)
            other = jnp.where(row == 0, -1, pltpu.roll(here, 1, axis=0))
            moved = jnp.where(lane < -d, other, here)
        else:
            here = pltpu.roll(tok, span - d, axis=1)
            other = jnp.where(row == count - 1, -1, pltpu.roll(here, count - 1, axis=0))
            moved = jnp.where(lane >= span - d, other, here)
        shifted[d + 3] = moved

    values = lax.broadcasted_iota(jnp.int32, (vocab, span), 0)

    def onehot(c, sign):
        found = []
        for j in range(4):
            token = shifted[3 + (j - 3) * sign, pl.ds(c, 1), :]
            found.append(jnp.where(values == token, 1.0, 0.0))
        one = jnp.concatenate(found, axis=0).astype(BF16)
        return jnp.concatenate([one, one], axis=0)

    first_head = pl.multiple_of(core * (heads // 2), heads // 2)
    first_row = pl.multiple_of(core * rows, rows)
    some = pl.ds(first_head, heads // 2)

    def remote(i, slot, run):
        rev = i >= base
        b = rev.astype(jnp.int32)
        c = jnp.clip(jnp.where(rev, i + 2, base - 1 - i), 0, count - 1)
        run = jnp.where(i == base, 0.0, run)
        dist = within[1 - b, c, some] + run
        decay = jnp.exp(-rate_ref[b, some] * dist)
        one = onehot(c, 1 - 2 * b)
        x = convolve(conv_ref[b, pl.ds(first_row, rows), :], one)
        x = x.reshape(heads // 2, head, span) * decay[:, None, :]
        x_held[slot] = x.reshape(rows, span).astype(BF16)
        bt = convolve(conv_ref[b, inner : inner + width, :], one)
        ahead = jnp.where(rev, 0.0, bt)
        behind = jnp.where(jnp.logical_and(rev, i < count - 2), bt, 0.0)
        b_held[slot] = jnp.concatenate([ahead, behind], axis=0).astype(BF16)
        return run + total[c, some]

    def gather(g, run, first):
        for k in range(group):
            run = remote(g * group + k, k, run)
        part = jnp.zeros((rows, 2 * width), F32)
        for k in range(group):
            part = part + dot(x_held[k], b_held[k], NT)
        state[...] = part if first else state[...] + part
        return run

    run = gather(0, jnp.zeros((heads // 2, span), F32), True)
    if count - 2 > group:
        lax.fori_loop(1, pl.cdiv(count - 2, group), lambda g, run: gather(g, run, False), run)

    stacked = (heads // 2, head, width)
    through, added = [], []
    for b in range(2):
        c = base + b
        one = onehot(c, 1 - 2 * b)
        decay = jnp.exp(-rate_ref[b, some] * within[1 - b, c, some])
        x = convolve(conv_ref[b, pl.ds(first_row, rows), :], one)
        x = x.reshape(heads // 2, head, span) * decay[:, None, :]
        bt = convolve(conv_ref[b, inner : inner + width, :], one)
        added.append(dot(x.reshape(rows, span).astype(BF16), bt.astype(BF16), NT))
        whole = jnp.exp(-rate_ref[b, some] * total[c, some])
        through.append(whole[:, None, :width])
    ahead, behind = state[:, :width], state[:, width:]
    ahead_next = (ahead.reshape(stacked) * through[0]).reshape(rows, width) + added[0]
    behind_next = (behind.reshape(stacked) * through[1]).reshape(rows, width) + added[1]
    first = jnp.concatenate([ahead, behind_next], axis=1).astype(BF16)
    second = jnp.concatenate([ahead_next, behind], axis=1).astype(BF16)
    mine_ref[...] = jnp.where(core == 0, first, second)
    mate_ref[...] = jnp.where(core == 0, second, first)

    onehot_ref[0] = onehot(me, 1)
    onehot_ref[1] = onehot(me, -1)


def own_kernel(
    onehot_ref, conv_ref, decay_ref,
    y_ref, x_ref, scores_ref, c_ref,
):
    inner = y_ref.shape[0]
    width = c_ref.shape[1]
    heads = decay_ref.shape[1]
    head = inner // heads
    for b in range(2):
        conv = convolve(conv_ref[b], onehot_ref[b]).astype(BF16)
        ct = conv[inner + width :]
        c_ref[b] = ct
        scores = dot(conv[inner : inner + width], ct, TN).astype(BF16)
        if b == 1:
            x_ref[...] = conv[:inner]
            scores_ref[...] = scores
            break
        for h in range(heads):
            rows = slice(h * head, (h + 1) * head)
            y_ref[rows] = dot(conv[rows], scores * decay_ref[b, h])


def output_kernel(
    mine_ref, mate_ref, reach_ref, decay_ref,
    y_ref, x_ref, scores_ref, c_ref, gates_ref, hgt_ref, out_ref,
    mixed_hbm,
    state, carried, mixin, mixed, sems,
):
    heads, span = reach_ref.shape[1:]
    inner = y_ref.shape[0]
    width = c_ref.shape[1]
    head = inner // heads
    core = lax.axis_index("seq") & 1
    part = inner // 2
    state[pl.ds(pl.multiple_of(core * part, part), part)] = mine_ref[...]
    state[pl.ds(pl.multiple_of((1 - core) * part, part), part)] = mate_ref[...]
    for b in range(2):
        carried[b] = dot(state[:, b * width : (b + 1) * width], c_ref[b])
    for h in range(heads):
        rows = slice(h * head, (h + 1) * head)
        both = jnp.zeros((head, span), F32)
        for b in range(2):
            if b == 0:
                y = y_ref[rows]
            else:
                y = dot(x_ref[rows], scores_ref[...] * decay_ref[b, h])
            y = y + reach_ref[b, h : h + 1] * carried[b, rows]
            v = y * gates_ref[rows]
            inv = lax.rsqrt(jnp.sum(v * v, axis=0, keepdims=True) * (1.0 / head) + EPS)
            both = both + v * inv * hgt_ref[rows, b : b + 1]
        mixin[rows] = both.astype(BF16)
    columns = mixed.shape[1] // 4
    copies = []
    for k in range(4):
        cols = pl.ds(k * columns, columns)
        mixed[:, cols] = dot(out_ref[cols], mixin[...]).astype(BF16).T
        copies.append(pltpu.make_async_copy(mixed.at[:, cols], mixed_hbm.at[:, cols], sems.at[k]))
        copies[-1].start()
    for copy in copies:
        copy.wait()


def shards(
    ids, exponents, embedding, norm_gain, in_proj, conv_weight, conv_bias, rates, head_gain, out_proj
):
    count = lax.axis_size("seq")
    bits = count.bit_length() - 1
    heads, span = exponents.shape
    vocab = embedding.shape[0]
    inner = out_proj.shape[0]
    wide = conv_bias.shape[1]
    width = (wide - inner) // 2
    taps = conv_weight.shape[1]
    group = min(count - 2, 16)
    pin = lambda value: pltpu.with_memory_space_constraint(value, pltpu.HBM)
    vmem = pl.BlockSpec(memory_space=pltpu.VMEM)
    hbm = pl.BlockSpec(memory_space=pltpu.HBM)
    f32 = lambda *shape: jax.ShapeDtypeStruct(shape, F32)
    b16 = lambda *shape: jax.ShapeDtypeStruct(shape, BF16)

    packed = pl.pallas_call(
        pack_kernel,
        out_shape=jax.ShapeDtypeStruct((1, heads, span), jnp.int32),
        in_specs=[hbm, hbm],
        out_specs=vmem,
        scratch_shapes=[
            pltpu.VMEM((1, span), jnp.int32),
            pltpu.VMEM((heads, span), jnp.int32),
            pltpu.SemaphoreType.DMA((2,)),
        ],
        compiler_params=pltpu.CompilerParams(vmem_limit_bytes=MIB),
        name="pack",
    )(pin(ids[None, :]), pin(exponents))

    def swap(value, mask):
        return lax.ppermute(value, "seq", [(i, i ^ mask) for i in range(count)])

    stages = [[count // 2, count // 2 + count // 4, count // 4]]
    stages += [[1 << bit] for bit in reversed(range(bits - 2))]
    tables = pl.pallas_call(
        prep_kernel,
        out_shape=(
            b16(2, wide, 2 * taps * vocab),
            b16(*embedding.shape),
            f32(inner, LANES),
            f32(2, heads, span),
        ),
        in_specs=[hbm] * 7,
        out_specs=(vmem,) * 4,
        scratch_shapes=[
            pltpu.VMEM((2, heads), F32),
            pltpu.VMEM(embedding.shape, BF16),
            pltpu.VMEM((1, inner), F32),
            pltpu.VMEM((inner, wide), BF16),
            pltpu.VMEM(conv_weight.shape, F32),
            pltpu.VMEM(conv_bias.shape, F32),
            pltpu.VMEM(head_gain.shape, F32),
            pltpu.SemaphoreType.DMA((8,)),
        ],
        compiler_params=pltpu.CompilerParams(vmem_limit_bytes=16 * MIB),
        name="prep",
        cost_estimate=pl.CostEstimate(
            flops=100_000_000, bytes_accessed=12_000_000, transcendentals=2_000_000
        ),
    )(*map(pin, (rates, embedding, norm_gain[None, :], in_proj, conv_weight, conv_bias, head_gain)))

    held, masks = packed, [0]
    for k, stage in enumerate(stages[:-1]):
        held = jnp.concatenate([held] + [swap(held, mask) for mask in stage], axis=0)
        masks = masks + [m ^ mask for mask in stage for m in masks]
        if k == 0:
            held, tables = lax.optimization_barrier((held, tables))
            conv_table, norm_table, gain_table, rate_table = tables
            local = pl.pallas_call(
                local_kernel,
                out_shape=(b16(2, heads, span, span), f32(inner, span), f32(2, heads, span)),
                in_specs=[vmem] * 3 + [hbm],
                out_specs=(vmem,) * 3,
                scratch_shapes=[pltpu.VMEM((inner, inner), BF16), pltpu.SemaphoreType.DMA],
                compiler_params=pltpu.CompilerParams(vmem_limit_bytes=10 * MIB),
                name="local",
                cost_estimate=pl.CostEstimate(
                    flops=20_000_000, bytes_accessed=5_000_000, transcendentals=2_000_000
                ),
            )(held, rate_table, norm_table, pin(in_proj))
        if k == len(stages) - 2:
            held, local = lax.optimization_barrier((held, local))
    far = swap(held, 1)
    masks = masks + [m ^ 1 for m in masks]
    turned = pl.pallas_call(
        turn_kernel,
        out_shape=b16(*out_proj.shape[::-1]),
        in_specs=[hbm, vmem],
        out_specs=vmem,
        compiler_params=pltpu.CompilerParams(vmem_limit_bytes=4 * MIB),
        name="turn",
        cost_estimate=pl.CostEstimate(
            flops=40_000_000, bytes_accessed=6_000_000, transcendentals=0
        ),
    )(held, out_proj)

    decays, gates, reach = local
    mine, mate, onehots = pl.pallas_call(
        functools.partial(states_kernel, masks),
        out_shape=(
            b16(inner // 2, 2 * width), b16(inner // 2, 2 * width),
            b16(2, 2 * taps * vocab, span),
        ),
        in_specs=[vmem] * 4,
        out_specs=(vmem,) * 3,
        scratch_shapes=[
            pltpu.VMEM((2, count, heads, span), F32),
            pltpu.VMEM((count, heads, span), F32),
            pltpu.VMEM((count, span), jnp.int32),
            pltpu.VMEM((7, count, span), jnp.int32),
            pltpu.VMEM((group, inner // 2, span), BF16),
            pltpu.VMEM((group, 2 * width, span), BF16),
            pltpu.VMEM((inner // 2, 2 * width), F32),
        ],
        compiler_params=pltpu.CompilerParams(vmem_limit_bytes=(20 if count <= 32 else 32) * MIB),
        name="states",
        cost_estimate=pl.CostEstimate(
            flops=10_000_000_000, bytes_accessed=4_000_000, transcendentals=3_000_000
        ),
    )(held, far, conv_table, rate_table)
    mate = swap(mate, 1)
    own = pl.pallas_call(
        own_kernel,
        out_shape=(
            f32(inner, span), b16(inner, span), b16(span, span),
            b16(2, width, span),
        ),
        in_specs=[vmem] * 3,
        out_specs=(vmem,) * 4,
        compiler_params=pltpu.CompilerParams(vmem_limit_bytes=12 * MIB),
        name="own",
        cost_estimate=pl.CostEstimate(
            flops=3_000_000_000, bytes_accessed=9_000_000, transcendentals=1_000_000
        ),
    )(onehots, conv_table, decays)
    return pl.pallas_call(
        output_kernel,
        out_shape=b16(span, inner),
        in_specs=[vmem] * 11,
        out_specs=hbm,
        scratch_shapes=[
            pltpu.VMEM((inner, 2 * width), BF16),
            pltpu.VMEM((2, inner, span), F32),
            pltpu.VMEM((inner, span), BF16),
            pltpu.VMEM((span, inner), BF16),
            pltpu.SemaphoreType.DMA((4,)),
        ],
        compiler_params=pltpu.CompilerParams(vmem_limit_bytes=14 * MIB),
        name="output",
        cost_estimate=pl.CostEstimate(
            flops=2_000_000_000, bytes_accessed=6_000_000, transcendentals=100_000
        ),
    )(
        mine, mate, reach, decays, *own, gates, gain_table, turned,
    )


def solution(mesh):
    in_specs = (
        P(("parts", "seq")),
        P(None, ("parts", "seq")),
        P(), P(), P(), P(), P(), P(), P(), P(),
    )
    out_specs = P(("parts", "seq"), None)
    return jax.shard_map(shards, mesh=mesh, in_specs=in_specs, out_specs=out_specs, check_vma=False)
```

time: 25.5 us -> 24.1 us (0.945)
  waiting for transfers between devices: 4.75 us -> 3.24 us
  starting transfers between devices: 7.17 us -> 7.46 us
    ppermute x5 -> x6, waiting for transfers between devices: 4.75 us -> 3.24 us  [swap(): return lax.ppermute(value, 'seq', [(i, i ^ mask) for i in range(count)])]
    pallas_call x1 -> x5, Pallas kernels: 8.42 us -> 9.89 us  [the longest x1 3.11 us: shards(): pl.pallas_call(functools.partial(states_kernel, masks), out_shape=(b16(in...]
    pallas_call x1, Pallas kernels: 3.86 us -> 2.43 us  [shards(): pl.pallas_call(prep_kernel, out_shape=(b16(2, wide, 2 * taps * vocab), b1...]
    ppermute x5 -> x6, starting transfers between devices: 7.17 us -> 7.46 us  [swap(): return lax.ppermute(value, 'seq', [(i, i ^ mask) for i in range(count)])]
  transfers between devices with their start and end apart: 5 -> 6, of which waited for: 3 -> 4; matrix products, arithmetic and copies ran while one was open for 0% -> 0% of each run, Pallas kernels for 15% -> 28%
where the time goes in v2:
time: 24.1 us; the launch traced here: 23.9 us
  Pallas kernels  13.1 us (54%)
  starting transfers between devices  7.46 us (31%)
  waiting for transfers between devices  3.24 us (13%)
    ppermute x6, starting transfers between devices, swap(): return lax.ppermute(value, 'seq', [(i, i ^ mask) for i in range(count)])  7.46 us
    ppermute x6, waiting for transfers between devices, swap(): return lax.ppermute(value, 'seq', [(i, i ^ mask) for i in range(count)])  3.24 us
    pallas_call x1, Pallas kernels, shards(): pl.pallas_call(functools.partial(states_kernel, masks), out_shape=(b16(in...  3.11 us
    pallas_call x1, Pallas kernels, shards(): pl.pallas_call(output_kernel, out_shape=b16(span, inner), in_specs=[vmem]...  2.47 us
    pallas_call x1, Pallas kernels, shards(): pl.pallas_call(prep_kernel, out_shape=(b16(2, wide, 2 * taps * vocab), b1...  2.43 us
    pallas_call x1, Pallas kernels, shards(): pl.pallas_call(local_kernel, out_shape=(b16(2, heads, span, span), f32(in...  2.32 us
    pallas_call x1, Pallas kernels, shards(): pl.pallas_call(own_kernel, out_shape=(f32(inner, span), b16(inner, span),...  1.35 us
    pallas_call x1, Pallas kernels, shards(): pl.pallas_call(pack_kernel, out_shape=jax.ShapeDtypeStruct((1, heads, spa...  0.75 us
  transfers between devices with their start and end apart: 6, of which 4 were waited for; matrix products, arithmetic and copies ran while one was open for 0% of the time, Pallas kernels for 28%

profile of v2, /device:TPU:0, one launch (start us, length us, event | category | flops | bytes accessed | tf_op | source)
XLA Modules:
  0.0 23.9 jit_solution(17922357105290125305)
XLA Ops:
  0.0 0.8 %pack.1 = s32[1,16,256]{2,1,0:T(8,128)S(1)} custom-call(s32[1,256]{1,0:T(1,128)} %bitcast.3, s32[16,256]{1,0:T(8,128)} %exp_ref.1), custom_call_target="tpu_custom_call" | custom-call | tf_op jit(solution)/shard_map/pack/pallas_call | solution.py:357
  0.8 3.1 %collective-permute-start.2 = (s32[1,16,256]{2,1,0:T(8,128)S(1)}, s32[1,16,256]{2,1,0:T(8,128)S(1)}, u32[]{:S(2)}, u32[]{:S(2)}) collective-permute-start(s32[1,16,256]{2,1,0:T(8,128)S(1)} %pack.1), channel_id=1, source_target_pairs={{0,4},{1,5},{2,6},{3,7},{4,0},{5,1},{6,2},{7,3},{8,12},{9,13},{10,... | collective-permute-start | bytes 49160 | tf_op jit(solution)/shard_map/ppermute | solution.py:372
  3.9 2.5 %collective-permute-start.1 = (s32[1,16,256]{2,1,0:T(8,128)S(1)}, s32[1,16,256]{2,1,0:T(8,128)S(1)}, u32[]{:S(2)}, u32[]{:S(2)}) collective-permute-start(s32[1,16,256]{2,1,0:T(8,128)S(1)} %pack.1), channel_id=1, source_target_pairs={{0,12},{1,13},{2,14},{3,15},{4,8},{5,9},{6,10},{7,11},{8,4},{9,5},... | collective-permute-start | bytes 49160 | tf_op jit(solution)/shard_map/ppermute | solution.py:372
  6.3 0.1 collective-permute-start
  6.4 0.0 copy-start
  6.4 2.4 %prep.1 = (bf16[2,1280,128]{2,1,0:T(8,128)(2,1)S(1)}, bf16[16,1024]{1,0:T(8,128)(2,1)S(1)}, f32[1024,128]{1,0:T(8,128)S(1)}, f32[2,16,256]{2,1,0:T(8,128)S(1)}) custom-call(f32[2,16]{1,0:T(2,128)} %rates_hbm.1, bf16[16,1024]{1,0:T(8,128)(2,1)} %emb_hbm.1, f32[1,1024]{1,0:T(1,128)} %bitcast.2, bf16[1024,2304]{1,0:T(8,128)(2,1)} %in_hbm.3, ...), custom_call_target="tpu_custom_call" | custom-call | flops 100000000 | bytes 12000000 | tf_op jit(solution)/shard_map/prep/pallas_call | solution.py:376
  8.9 0.0 collective-permute-done.2
  8.9 0.7 %collective-permute-done.1 = s32[1,16,256]{2,1,0:T(8,128)S(1)} collective-permute-done((s32[1,16,256]{2,1,0:T(8,128)S(1)}, s32[1,16,256]{2,1,0:T(8,128)S(1)}, u32[]{:S(2)}, u32[]{:S(2)}) %collective-permute-start.1) | collective-permute-done | bytes 16416 | tf_op jit(solution)/shard_map/ppermute | solution.py:372
  9.6 1.4 %collective-permute-done = s32[1,16,256]{2,1,0:T(8,128)S(1)} collective-permute-done((s32[1,16,256]{2,1,0:T(8,128)S(1)}, s32[1,16,256]{2,1,0:T(8,128)S(1)}, u32[]{:S(2)}, u32[]{:S(2)}) %collective-permute-start) | collective-permute-done | bytes 16416 | tf_op jit(solution)/shard_map/ppermute | solution.py:372
  11.0 1.5 %collective-permute-start.3 = (s32[4,16,256]{2,1,0:T(8,128)S(1)}, s32[4,16,256]{2,1,0:T(8,128)S(1)}, u32[]{:S(2)}, u32[]{:S(2)}) collective-permute-start(s32[4,16,256]{2,1,0:T(8,128)S(1)} %pad_add_fusion.1.held_ref), channel_id=1, source_target_pairs={{0,2},{1,3},{2,0},{3,1},{4,6},{5,7},{6,4},{7,5},{8,10},{9,11},{10,... | collective-permute-start | bytes 196616 | tf_op jit(solution)/shard_map/ppermute | solution.py:372
  12.5 2.3 %local.1 = (bf16[2,16,256,256]{3,2,1,0:T(8,128)(2,1)S(1)}, f32[1024,256]{1,0:T(8,128)S(1)}, f32[2,16,256]{2,1,0:T(8,128)S(1)}) custom-call(s32[4,16,256]{2,1,0:T(8,128)S(1)} %pad_add_fusion.1.held_ref, f32[2,16,256]{2,1,0:T(8,128)S(1)} %get-tuple-element.33.rate_ref, bf16[16,1024]{1,0:T(8,128)(2,1)S(1)} %get-tuple-element.34.norm_ref, bf16[1024,2304]{1,0:T(8,128)(2,1)} %in_hbm.3), custom_call_target="tpu_custom_call" | custom-call | flops 20000000 | bytes 5000000 | tf_op jit(solution)/shard_map/local/pallas_call | solution.py:410
  14.8 0.4 %collective-permute-done.3 = s32[4,16,256]{2,1,0:T(8,128)S(1)} collective-permute-done((s32[4,16,256]{2,1,0:T(8,128)S(1)}, s32[4,16,256]{2,1,0:T(8,128)S(1)}, u32[]{:S(2)}, u32[]{:S(2)}) %collective-permute-start.3) | collective-permute-done | bytes 65568 | tf_op jit(solution)/shard_map/ppermute | solution.py:372
  15.3 0.1 collective-permute-start.4
  15.3 0.0 copy-done
  15.4 0.6 %turn.1.out_ref = bf16[1024,1024]{1,0:T(8,128)(2,1)S(1)} custom-call(s32[8,16,256]{2,1,0:T(8,128)S(1)} %pad_add_fusion.near_ref, bf16[1024,1024]{1,0:T(8,128)(2,1)S(1)} %copy-done), custom_call_target="tpu_custom_call" | custom-call | flops 40000000 | bytes 6000000 | tf_op jit(solution)/shard_map/turn/pallas_call | solution.py:426
  16.0 0.7 %collective-permute-done.4.far_ref = s32[8,16,256]{2,1,0:T(8,128)S(1)} collective-permute-done((s32[8,16,256]{2,1,0:T(8,128)S(1)}, s32[8,16,256]{2,1,0:T(8,128)S(1)}, u32[]{:S(2)}, u32[]{:S(2)}) %collective-permute-start.4) | collective-permute-done | bytes 131104 | tf_op jit(solution)/shard_map/ppermute | solution.py:372
  16.7 3.1 %states.1 = (bf16[512,256]{1,0:T(8,128)(2,1)S(1)}, bf16[512,256]{1,0:T(8,128)(2,1)S(1)}, bf16[2,128,256]{2,1,0:T(8,128)(2,1)S(1)}) custom-call(s32[8,16,256]{2,1,0:T(8,128)S(1)} %pad_add_fusion.near_ref, s32[8,16,256]{2,1,0:T(8,128)S(1)} %collective-permute-done.4.far_ref, bf16[2,1280,128]{2,1,0:T(8,128)(2,1)S(1)} %get-tuple-element.39.conv_ref, ...), custom_call_target="tpu_custom_call" | custom-call | flops 10000000000 | bytes 4000000 | tf_op jit(solution)/shard_map/states/pallas_call | solution.py:439
  19.8 0.2 collective-permute-start.5
  20.0 1.4 %own.1 = (f32[1024,256]{1,0:T(8,128)S(1)}, bf16[1024,256]{1,0:T(8,128)(2,1)S(1)}, bf16[256,256]{1,0:T(8,128)(2,1)S(1)}, bf16[2,128,256]{2,1,0:T(8,128)(2,1)S(1)}) custom-call(bf16[2,128,256]{2,1,0:T(8,128)(2,1)S(1)} %get-tuple-element.44.onehot_ref, bf16[2,1280,128]{2,1,0:T(8,128)(2,1)S(1)} %get-tuple-element.39.conv_ref, ...), custom_call_target="tpu_custom_call" | custom-call | flops 3000000000 | bytes 9000000 | tf_op jit(solution)/shard_map/own/pallas_call | solution.py:463
  21.4 0.0 collective-permute-done.5.mate_ref
  21.4 2.5 %output.1 = bf16[256,1024]{1,0:T(8,128)(2,1)} custom-call(bf16[512,256]{1,0:T(8,128)(2,1)S(1)} %get-tuple-element.40.mine_ref, bf16[512,256]{1,0:T(8,128)(2,1)S(1)} %collective-permute-done.5.mate_ref, f32[2,16,256]{2,1,0:T(8,128)S(1)} %get-tuple-element.42.reach_ref, bf16[2,16,256,256]{3,2,1,0:T(8,128)(2,1)S(1)} %get-tuple-element.43.decay_ref, ...), custom_call_target="tpu_custom_call" | custom-call | flops 2000000000 | bytes 6000000 | tf_op jit(solution)/shard_map/output/pallas_call | solution.py:477
  (2 shorter events, 0.0 us)
Async XLA Ops:
  0.8 8.1 %collective-permute-start.2 = (s32[1,16,256]{2,1,0:T(8,128)S(1)}, s32[1,16,256]{2,1,0:T(8,128)S(1)}, u32[]{:S(2)}, u32[]{:S(2)}) collective-permute-start(s32[1,16,256]{2,1,0:T(8,128)S(1)} %pack.1), channel_id=1, source_target_pairs={{0,4},{1,5},{2,6},{3,7},{4,0},{5,1},{6,2},{7,3},{8,12},{9,13},{10,... | collective-permute-start | bytes 49160 | tf_op jit(solution)/shard_map/ppermute | solution.py:372
  3.9 5.8 %collective-permute-start.1 = (s32[1,16,256]{2,1,0:T(8,128)S(1)}, s32[1,16,256]{2,1,0:T(8,128)S(1)}, u32[]{:S(2)}, u32[]{:S(2)}) collective-permute-start(s32[1,16,256]{2,1,0:T(8,128)S(1)} %pack.1), channel_id=1, source_target_pairs={{0,12},{1,13},{2,14},{3,15},{4,8},{5,9},{6,10},{7,11},{8,4},{9,5},... | collective-permute-start | bytes 49160 | tf_op jit(solution)/shard_map/ppermute | solution.py:372
  6.3 4.6 %collective-permute-start = (s32[1,16,256]{2,1,0:T(8,128)S(1)}, s32[1,16,256]{2,1,0:T(8,128)S(1)}, u32[]{:S(2)}, u32[]{:S(2)}) collective-permute-start(s32[1,16,256]{2,1,0:T(8,128)S(1)} %pack.1), channel_id=1, source_target_pairs={{0,8},{1,9},{2,10},{3,11},{4,12},{5,13},{6,14},{7,15},{8,0},{9,1},... | collective-permute-start | bytes 49160 | tf_op jit(solution)/shard_map/ppermute | solution.py:372
  6.4 8.9 %copy-start = (bf16[1024,1024]{1,0:T(8,128)(2,1)S(1)}, bf16[1024,1024]{1,0:T(8,128)(2,1)}, u32[]{:S(2)}) copy-start(bf16[1024,1024]{1,0:T(8,128)(2,1)} %out_ref.1) | copy-start | bytes 6291460
  11.0 4.3 %collective-permute-start.3 = (s32[4,16,256]{2,1,0:T(8,128)S(1)}, s32[4,16,256]{2,1,0:T(8,128)S(1)}, u32[]{:S(2)}, u32[]{:S(2)}) collective-permute-start(s32[4,16,256]{2,1,0:T(8,128)S(1)} %pad_add_fusion.1.held_ref), channel_id=1, source_target_pairs={{0,2},{1,3},{2,0},{3,1},{4,6},{5,7},{6,4},{7,5},{8,10},{9,11},{10,... | collective-permute-start | bytes 196616 | tf_op jit(solution)/shard_map/ppermute | solution.py:372
  15.3 1.4 %collective-permute-start.4 = (s32[8,16,256]{2,1,0:T(8,128)S(1)}, s32[8,16,256]{2,1,0:T(8,128)S(1)}, u32[]{:S(2)}, u32[]{:S(2)}) collective-permute-start(s32[8,16,256]{2,1,0:T(8,128)S(1)} %pad_add_fusion.near_ref), channel_id=1, source_target_pairs={{0,1},{1,0},{2,3},{3,2},{4,5},{5,4},{6,7},{7,6},{8,9},{9,8},{10,11... | collective-permute-start | bytes 393224 | tf_op jit(solution)/shard_map/ppermute | solution.py:372
  19.8 1.6 %collective-permute-start.5 = (bf16[512,256]{1,0:T(8,128)(2,1)S(1)}, bf16[512,256]{1,0:T(8,128)(2,1)S(1)}, u32[]{:S(2)}, u32[]{:S(2)}) collective-permute-start(bf16[512,256]{1,0:T(8,128)(2,1)S(1)} %get-tuple-element.41), channel_id=1, source_target_pairs={{0,1},{1,0},{2,3},{3,2},{4,5},{5,4},{6,7},{7,6},{8,9},{9,8},{10,11... | collective-permute-start | bytes 786440 | tf_op jit(solution)/shard_map/ppermute | solution.py:372

commit v3 on v2

--- a/solution.py
+++ b/solution.py
@@ -159,6 +159,25 @@
     return pre, tot - inc, tot
 
 
+def shift_tokens(ids, shifted):
+    tok = ids[...]
+    count, span = tok.shape
+    lane = lax.broadcasted_iota(jnp.int32, tok.shape, 1)
+    row = lax.broadcasted_iota(jnp.int32, tok.shape, 0)
+    for d in range(-3, 4):
+        if d == 0:
+            moved = tok
+        elif d < 0:
+            here = pltpu.roll(tok, -d, axis=1)
+            other = jnp.where(row == 0, -1, pltpu.roll(here, 1, axis=0))
+            moved = jnp.where(lane < -d, other, here)
+        else:
+            here = pltpu.roll(tok, span - d, axis=1)
+            other = jnp.where(row == count - 1, -1, pltpu.roll(here, count - 1, axis=0))
+            moved = jnp.where(lane >= span - d, other, here)
+        shifted[d + 3] = moved
+
+
 def turn_kernel(near_ref, out_ref, turned_ref):
     turned_ref[...] = out_ref[...].T
 
@@ -190,22 +209,7 @@
             total[c] = tot[block]
             ids[pl.ds(c, 1), :] = ref[slot, 0:1] >> 16
 
-    tok = ids[...]
-    lane = lax.broadcasted_iota(jnp.int32, tok.shape, 1)
-    row = lax.broadcasted_iota(jnp.int32, tok.shape, 0)
-    for d in range(-3, 4):
-        if d == 0:
-            moved = tok
-        elif d < 0:
-            here = pltpu.roll(tok, -d, axis=1)
-            other = jnp.where(row == 0, -1, pltpu.roll(here, 1, axis=0))
-            moved = jnp.where(lane < -d, other, here)
-        else:
-            here = pltpu.roll(tok, span - d, axis=1)
-            other = jnp.where(row == count - 1, -1, pltpu.roll(here, count - 1, axis=0))
-            moved = jnp.where(lane >= span - d, other, here)
-        shifted[d + 3] = moved
-
+    shift_tokens(ids, shifted)
     values = lax.broadcasted_iota(jnp.int32, (vocab, span), 0)
 
     def onehot(c, sign):
@@ -272,6 +276,156 @@
 
     onehot_ref[0] = onehot(me, 1)
     onehot_ref[1] = onehot(me, -1)
+
+
+def spans_kernel(
+    first, masks, held_ref, conv_ref, rate_ref, state_ref, within_ref, total_ref, x_held, b_held
+):
+    heads, span = held_ref.shape[1:]
+    count, inner, width = state_ref.shape
+    head = inner // heads
+    vocab = conv_ref.shape[2] // 8
+    me = lax.axis_index("seq")
+    pre, post, tot = unpack(held_ref[first : first + count].reshape(count * heads, span))
+    within_ref[0] = pre.reshape(count, heads, span)
+    within_ref[1] = post.reshape(count, heads, span)
+    total_ref[...] = tot.reshape(count, heads, span)
+    lane = lax.broadcasted_iota(jnp.int32, (heads, span), 1)
+    values = lax.broadcasted_iota(jnp.int32, (vocab, span), 0)
+    for k, mask in enumerate(masks):
+        rev = (jnp.bitwise_xor(me, mask) > me) if mask else (me & 1) == 1
+        b = rev.astype(jnp.int32)
+        token = jnp.broadcast_to(held_ref[first + k, 0:1] >> 16, (vocab, span))
+        found = []
+        for far in (3, 2, 1, 0):
+            there = token
+            if far:
+                there = jnp.where(rev, pltpu.roll(token, span - far, 1), pltpu.roll(token, far, 1))
+            found.append(jnp.where(values == there, 1.0, 0.0))
+        one = jnp.concatenate(found, axis=0).astype(BF16)
+        one = jnp.concatenate([one, one], axis=0)
+        rows = slice(k * heads, (k + 1) * heads)
+        decay = jnp.exp(-rate_ref[b] * jnp.where(rev, pre[rows], post[rows]))
+        decay = jnp.where(jnp.where(rev, span - 1 - lane, lane) < 3, 0.0, decay)
+        x = convolve(conv_ref[b, :inner, :], one).reshape(heads, head, span) * decay[:, None, :]
+        bt = convolve(conv_ref[b, inner : inner + width, :], one)
+        x_held[k] = x.reshape(inner, span).astype(BF16)
+        b_held[k] = bt.astype(BF16)
+    for k in range(count):
+        for r in range(0, inner, 512):
+            state_ref[k, r : r + 512] = dot(x_held[k, r : r + 512], b_held[k], NT)
+
+
+def combine_kernel(
+    masks,
+    held_ref, far_ref, state_a, within_a, total_a, state_b, within_b, total_b, conv_ref, rate_ref,
+    mine_ref, mate_ref, onehot_ref,
+    totals, between, ids, shifted,
+):
+    count = 2 * len(masks)
+    heads, span = held_ref.shape[1:]
+    first, inner, width = state_a.shape
+    head = inner // heads
+    vocab = conv_ref.shape[2] // 8
+    me = lax.axis_index("seq")
+    core = me & 1
+    base = me - core
+    parts = [(state_a, within_a, total_a, k) for k in range(first)]
+    parts += [(state_b, within_b, total_b, k) for k in range(len(masks) - first)]
+
+    far_e = ((far_ref[...].reshape(len(masks) * heads, span) & 0xFFFF) + 1).astype(F32)
+    far_tot = jnp.broadcast_to(jnp.sum(far_e, axis=1, keepdims=True), (len(masks) * heads, LANES))
+    for slot, mask in enumerate(masks):
+        c = jnp.bitwise_xor(me, mask)
+        _, _, tot, k = parts[slot]
+        totals[c] = tot[k, :, :LANES]
+        ids[pl.ds(c, 1), :] = held_ref[slot, 0:1] >> 16
+        c = jnp.bitwise_xor(c, 1)
+        totals[c] = far_tot[slot * heads : (slot + 1) * heads]
+        ids[pl.ds(c, 1), :] = far_ref[slot, 0:1] >> 16
+    run = jnp.zeros((heads, LANES), F32)
+    for i in range(count - 2):
+        c = jnp.where(i >= base, i + 2, base - 1 - i)
+        run = jnp.where(i == base, 0.0, run)
+        between[c] = run
+        run = run + totals[c]
+    between[me] = jnp.zeros((heads, LANES), F32)
+
+    shift_tokens(ids, shifted)
+    values = lax.broadcasted_iota(jnp.int32, (vocab, span), 0)
+    for b in range(2):
+        found = []
+        for j in range(4):
+            token = shifted[j if b == 0 else 6 - j, pl.ds(me, 1), :]
+            found.append(jnp.where(values == token, 1.0, 0.0))
+        one = jnp.concatenate(found, axis=0).astype(BF16)
+        onehot_ref[b] = jnp.concatenate([one, one], axis=0)
+
+    lane = lax.broadcasted_iota(jnp.int32, (1, span), 1)
+    token = jnp.full((8, span), -1, jnp.int32)
+    kind = jnp.full((1, span), -1, jnp.int32)
+    side = jnp.full((1, span), -1, jnp.int32)
+    dist = jnp.zeros((heads, LANES), F32)
+    rate = jnp.zeros((heads, LANES), F32)
+    scales = []
+    for slot, mask in enumerate(masks):
+        c = jnp.bitwise_xor(me, mask)
+        rev = (c > me) if mask else core == 1
+        b = rev.astype(jnp.int32)
+        here = jnp.logical_and(lane >= 8 * slot, lane < 8 * slot + 3)
+        near = here[:, :LANES]
+        taps = jnp.concatenate(
+            [shifted[3 + (j - 3) * (1 - 2 * b), pl.ds(c, 1), :] for j in (0, 1, 2, 3, 0, 1, 2, 3)],
+            axis=0,
+        )
+
+        def moved(ahead, behind):
+            start = ahead if slot == 0 else pltpu.roll(ahead, 8 * slot, 1)
+            return jnp.where(rev, pltpu.roll(behind, 8 * slot + 3, 1), start)
+
+        token = jnp.where(here, moved(taps, taps), token)
+        side = jnp.where(here, b, side)
+        kind = jnp.where(here, b if mask else 2, kind)
+        _, within, _, k = parts[slot]
+        gap = moved(within[1, k], within[0, k])[:, :LANES] + between[c]
+        dist = jnp.where(near, gap, dist)
+        rate = jnp.where(near, rate_ref[b, :, :LANES], rate)
+        scale = jnp.exp(-rate_ref[b, :, :LANES] * between[c])
+        scales.append((jnp.where(rev, 0.0, scale), jnp.where(rev, scale, 0.0)))
+    values = values[:, :LANES]
+    found = [jnp.where(values == token[j : j + 1, :LANES], 1.0, 0.0) for j in range(4)]
+    one = jnp.concatenate(found, axis=0)
+    side, kind = side[:, :LANES], kind[:, :LANES]
+    ones = [jnp.where(side == b, one, 0.0).astype(BF16) for b in (0, 0, 1, 1)]
+    table = jnp.concatenate(
+        [conv_ref[0, : inner + width, :], conv_ref[1, : inner + width, :]], axis=1
+    )
+    conv = convolve(table, jnp.concatenate(ones, axis=0))
+    x = conv[:inner].reshape(heads, head, LANES) * jnp.exp(-rate * dist)[:, None, :]
+    bt = conv[inner:]
+    bt = jnp.concatenate([jnp.where(kind == i, bt, 0.0) for i in range(3)], axis=0)
+    edges = dot(x.reshape(inner, LANES).astype(BF16), bt.astype(BF16), NT)
+
+    through = [jnp.exp(-rate_ref[b, :, :LANES] * totals[base + b]) for b in range(2)]
+    for h in range(heads):
+        rows = slice(h * head, (h + 1) * head)
+        ahead, behind = edges[rows, :width], edges[rows, width : 2 * width]
+        own = edges[rows, 2 * width :]
+        for slot, mask in enumerate(masks):
+            state, _, _, k = parts[slot]
+            value = state[k, rows]
+            if not mask:
+                own = own + value
+                continue
+            ahead = ahead + value * scales[slot][0][h : h + 1]
+            behind = behind + value * scales[slot][1][h : h + 1]
+        ahead_next = ahead * through[0][h : h + 1]
+        behind_next = behind * through[1][h : h + 1]
+        zero = core == 0
+        mine_ref[rows, :width] = jnp.where(zero, ahead, ahead_next)
+        mine_ref[rows, width:] = jnp.where(zero, behind_next, behind)
+        mate_ref[rows, :width] = jnp.where(zero, ahead_next + own, ahead).astype(BF16)
+        mate_ref[rows, width:] = jnp.where(zero, behind, behind_next + own).astype(BF16)
 
 
 def own_kernel(
@@ -297,6 +451,7 @@
 
 
 def output_kernel(
+    summed,
     mine_ref, mate_ref, reach_ref, decay_ref,
     y_ref, x_ref, scores_ref, c_ref, gates_ref, hgt_ref, out_ref,
     mixed_hbm,
@@ -308,8 +463,11 @@
     head = inner // heads
     core = lax.axis_index("seq") & 1
     part = inner // 2
-    state[pl.ds(pl.multiple_of(core * part, part), part)] = mine_ref[...]
-    state[pl.ds(pl.multiple_of((1 - core) * part, part), part)] = mate_ref[...]
+    if summed:
+        state[...] = (mine_ref[...] + mate_ref[...].astype(F32)).astype(BF16)
+    else:
+        state[pl.ds(pl.multiple_of(core * part, part), part)] = mine_ref[...]
+        state[pl.ds(pl.multiple_of((1 - core) * part, part), part)] = mate_ref[...]
     for b in range(2):
         carried[b] = dot(state[:, b * width : (b + 1) * width], c_ref[b])
     for h in range(heads):
@@ -400,65 +558,113 @@
         ),
     )(*map(pin, (rates, embedding, norm_gain[None, :], in_proj, conv_weight, conv_bias, head_gain)))
 
-    held, masks = packed, [0]
+    conv_table, norm_table, gain_table, rate_table = tables
+    local = pl.pallas_call(
+        local_kernel,
+        out_shape=(b16(2, heads, span, span), f32(inner, span), f32(2, heads, span)),
+        in_specs=[vmem] * 3 + [hbm],
+        out_specs=(vmem,) * 3,
+        scratch_shapes=[pltpu.VMEM((inner, inner), BF16), pltpu.SemaphoreType.DMA],
+        compiler_params=pltpu.CompilerParams(vmem_limit_bytes=10 * MIB),
+        name="local",
+        cost_estimate=pl.CostEstimate(
+            flops=20_000_000, bytes_accessed=5_000_000, transcendentals=2_000_000
+        ),
+    )(packed, rate_table, norm_table, pin(in_proj))
+
+    def spans(first, some, held):
+        many = len(some)
+        return pl.pallas_call(
+            functools.partial(spans_kernel, first, some),
+            out_shape=(
+                f32(many, inner, width), f32(2, many, heads, span), f32(many, heads, span),
+            ),
+            in_specs=[vmem] * 3,
+            out_specs=(vmem,) * 3,
+            scratch_shapes=[
+                pltpu.VMEM((many, inner, span), BF16), pltpu.VMEM((many, width, span), BF16),
+            ],
+            compiler_params=pltpu.CompilerParams(vmem_limit_bytes=12 * MIB),
+            name="spans",
+            cost_estimate=pl.CostEstimate(
+                flops=2_000_000_000, bytes_accessed=4_000_000, transcendentals=1_000_000
+            ),
+        )(held, conv_table, rate_table)
+
+    def turn(value):
+        return pl.pallas_call(
+            turn_kernel,
+            out_shape=b16(*out_proj.shape[::-1]),
+            in_specs=[hbm, vmem],
+            out_specs=vmem,
+            compiler_params=pltpu.CompilerParams(vmem_limit_bytes=4 * MIB),
+            name="turn",
+            cost_estimate=pl.CostEstimate(
+                flops=40_000_000, bytes_accessed=6_000_000, transcendentals=0
+            ),
+        )(value, out_proj)
+
+    summed = count == 16
+    held, masks, early = packed, [0], []
     for k, stage in enumerate(stages[:-1]):
-        held = jnp.concatenate([held] + [swap(held, mask) for mask in stage], axis=0)
+        if k == 1:
+            held, local = lax.optimization_barrier((held, local))
+        new = [swap(held, mask) for mask in stage]
+        if k == 1:
+            turned = turn(held)
+            if summed:
+                early.append(spans(0, masks, held))
+        held = jnp.concatenate([held] + new, axis=0)
         masks = masks + [m ^ mask for mask in stage for m in masks]
-        if k == 0:
-            held, tables = lax.optimization_barrier((held, tables))
-            conv_table, norm_table, gain_table, rate_table = tables
-            local = pl.pallas_call(
-                local_kernel,
-                out_shape=(b16(2, heads, span, span), f32(inner, span), f32(2, heads, span)),
-                in_specs=[vmem] * 3 + [hbm],
-                out_specs=(vmem,) * 3,
-                scratch_shapes=[pltpu.VMEM((inner, inner), BF16), pltpu.SemaphoreType.DMA],
-                compiler_params=pltpu.CompilerParams(vmem_limit_bytes=10 * MIB),
-                name="local",
-                cost_estimate=pl.CostEstimate(
-                    flops=20_000_000, bytes_accessed=5_000_000, transcendentals=2_000_000
-                ),
-            )(held, rate_table, norm_table, pin(in_proj))
-        if k == len(stages) - 2:
-            held, local = lax.optimization_barrier((held, local))
+        if k == 1:
+            held, early, turned = lax.optimization_barrier((held, early, turned))
     far = swap(held, 1)
-    masks = masks + [m ^ 1 for m in masks]
-    turned = pl.pallas_call(
-        turn_kernel,
-        out_shape=b16(*out_proj.shape[::-1]),
-        in_specs=[hbm, vmem],
-        out_specs=vmem,
-        compiler_params=pltpu.CompilerParams(vmem_limit_bytes=4 * MIB),
-        name="turn",
-        cost_estimate=pl.CostEstimate(
-            flops=40_000_000, bytes_accessed=6_000_000, transcendentals=0
-        ),
-    )(held, out_proj)
-
+    if summed:
+        early.append(spans(len(masks) // 2, masks[len(masks) // 2 :], held))
     decays, gates, reach = local
-    mine, mate, onehots = pl.pallas_call(
-        functools.partial(states_kernel, masks),
-        out_shape=(
-            b16(inner // 2, 2 * width), b16(inner // 2, 2 * width),
-            b16(2, 2 * taps * vocab, span),
-        ),
-        in_specs=[vmem] * 4,
-        out_specs=(vmem,) * 3,
-        scratch_shapes=[
-            pltpu.VMEM((2, count, heads, span), F32),
-            pltpu.VMEM((count, heads, span), F32),
-            pltpu.VMEM((count, span), jnp.int32),
-            pltpu.VMEM((7, count, span), jnp.int32),
-            pltpu.VMEM((group, inner // 2, span), BF16),
-            pltpu.VMEM((group, 2 * width, span), BF16),
-            pltpu.VMEM((inner // 2, 2 * width), F32),
-        ],
-        compiler_params=pltpu.CompilerParams(vmem_limit_bytes=(20 if count <= 32 else 32) * MIB),
-        name="states",
-        cost_estimate=pl.CostEstimate(
-            flops=10_000_000_000, bytes_accessed=4_000_000, transcendentals=3_000_000
-        ),
-    )(held, far, conv_table, rate_table)
+    if summed:
+        mine, mate, onehots = pl.pallas_call(
+            functools.partial(combine_kernel, masks),
+            out_shape=(f32(inner, 2 * width), b16(inner, 2 * width), b16(2, 2 * taps * vocab, span)),
+            in_specs=[vmem] * 10,
+            out_specs=(vmem,) * 3,
+            scratch_shapes=[
+                pltpu.VMEM((count, heads, LANES), F32),
+                pltpu.VMEM((count, heads, LANES), F32),
+                pltpu.VMEM((count, span), jnp.int32),
+                pltpu.VMEM((7, count, span), jnp.int32),
+            ],
+            compiler_params=pltpu.CompilerParams(vmem_limit_bytes=12 * MIB),
+            name="combine",
+            cost_estimate=pl.CostEstimate(
+                flops=1_000_000_000, bytes_accessed=8_000_000, transcendentals=300_000
+            ),
+        )(held, far, *early[0], *early[1], conv_table, rate_table)
+    else:
+        masks = masks + [m ^ 1 for m in masks]
+        mine, mate, onehots = pl.pallas_call(
+            functools.partial(states_kernel, masks),
+            out_shape=(
+                b16(inner // 2, 2 * width), b16(inner // 2, 2 * width),
+                b16(2, 2 * taps * vocab, span),
+            ),
+            in_specs=[vmem] * 4,
+            out_specs=(vmem,) * 3,
+            scratch_shapes=[
+                pltpu.VMEM((2, count, heads, span), F32),
+                pltpu.VMEM((count, heads, span), F32),
+                pltpu.VMEM((count, span), jnp.int32),
+                pltpu.VMEM((7, count, span), jnp.int32),
+                pltpu.VMEM((group, inner // 2, span), BF16),
+                pltpu.VMEM((group, 2 * width, span), BF16),
+                pltpu.VMEM((inner // 2, 2 * width), F32),
+            ],
+            compiler_params=pltpu.CompilerParams(vmem_limit_bytes=(20 if count <= 32 else 32) * MIB),
+            name="states",
+            cost_estimate=pl.CostEstimate(
+                flops=10_000_000_000, bytes_accessed=4_000_000, transcendentals=3_000_000
+            ),
+        )(held, far, conv_table, rate_table)
     mate = swap(mate, 1)
     own = pl.pallas_call(
         own_kernel,
@@ -475,7 +681,7 @@
         ),
     )(onehots, conv_table, decays)
     return pl.pallas_call(
-        output_kernel,
+        functools.partial(output_kernel, summed),
         out_shape=b16(span, inner),
         in_specs=[vmem] * 11,
         out_specs=hbm,

time: 24.1 us -> 23.4 us (0.971)
  waiting for transfers between devices: 3.24 us -> 0.73 us
  Pallas kernels: 13.1 us -> 14.3 us
  starting transfers between devices: 7.46 us -> 7.88 us
    ppermute x6, waiting for transfers between devices: 3.24 us -> 0.73 us  [swap(): return lax.ppermute(value, 'seq', [(i, i ^ mask) for i in range(count)])]
    pallas_call x3 -> x5, Pallas kernels: 6.21 us -> 7.55 us  [the longest x2 2.81 us: spans(): pl.pallas_call(functools.partial(spans_kernel, first, some), out_shape=(f...]
    ppermute x6, starting transfers between devices: 7.46 us -> 7.88 us  [swap(): return lax.ppermute(value, 'seq', [(i, i ^ mask) for i in range(count)])]
  transfers between devices with their start and end apart: 6 -> 6, of which waited for: 4 -> 2; matrix products, arithmetic and copies ran while one was open for 0% -> 0% of each run, Pallas kernels for 28% -> 41%
where the time goes in v3:
time: 23.4 us; the launch traced here: 23.2 us
  Pallas kernels  14.3 us (61%)
  starting transfers between devices  7.88 us (34%)
  waiting for transfers between devices  0.73 us (3%)
    ppermute x6, starting transfers between devices, swap(): return lax.ppermute(value, 'seq', [(i, i ^ mask) for i in range(count)])  7.88 us
    pallas_call x2, Pallas kernels, spans(): pl.pallas_call(functools.partial(spans_kernel, first, some), out_shape=(f...  2.81 us
    pallas_call x1, Pallas kernels, shards(): pl.pallas_call(functools.partial(output_kernel, summed), out_shape=b16(sp...  2.49 us
    pallas_call x1, Pallas kernels, shards(): pl.pallas_call(local_kernel, out_shape=(b16(2, heads, span, span), f32(in...  2.32 us
    pallas_call x1, Pallas kernels, shards(): pl.pallas_call(prep_kernel, out_shape=(b16(2, wide, 2 * taps * vocab), b1...  2.29 us
    pallas_call x1, Pallas kernels, shards(): pl.pallas_call(functools.partial(combine_kernel, masks), out_shape=(f32(i...  1.61 us
    pallas_call x1, Pallas kernels, shards(): pl.pallas_call(own_kernel, out_shape=(f32(inner, span), b16(inner, span),...  1.36 us
    pallas_call x1, Pallas kernels, shards(): pl.pallas_call(pack_kernel, out_shape=jax.ShapeDtypeStruct((1, heads, spa...  0.75 us
  transfers between devices with their start and end apart: 6, of which 2 were waited for; matrix products, arithmetic and copies ran while one was open for 0% of the time, Pallas kernels for 41%

profile of v3, /device:TPU:0, one launch (start us, length us, event | category | flops | bytes accessed | tf_op | source)
XLA Modules:
  0.0 23.2 jit_solution(2187546825149036919)
XLA Ops:
  0.0 0.8 %pack.1.held_ref = s32[1,16,256]{2,1,0:T(8,128)S(1)} custom-call(s32[1,256]{1,0:T(1,128)} %bitcast.3, s32[16,256]{1,0:T(8,128)} %exp_ref.1), custom_call_target="tpu_custom_call" | custom-call | tf_op jit(solution)/shard_map/pack/pallas_call | solution.py:515
  0.8 3.1 %collective-permute-start.2 = (s32[1,16,256]{2,1,0:T(8,128)S(1)}, s32[1,16,256]{2,1,0:T(8,128)S(1)}, u32[]{:S(2)}, u32[]{:S(2)}) collective-permute-start(s32[1,16,256]{2,1,0:T(8,128)S(1)} %pack.1.held_ref), channel_id=1, source_target_pairs={{0,4},{1,5},{2,6},{3,7},{4,0},{5,1},{6,2},{7,3},{8,12},{9,13},{10,... | collective-permute-start | bytes 49160 | tf_op jit(solution)/shard_map/ppermute | solution.py:530
  3.9 2.5 %collective-permute-start.1 = (s32[1,16,256]{2,1,0:T(8,128)S(1)}, s32[1,16,256]{2,1,0:T(8,128)S(1)}, u32[]{:S(2)}, u32[]{:S(2)}) collective-permute-start(s32[1,16,256]{2,1,0:T(8,128)S(1)} %pack.1.held_ref), channel_id=1, source_target_pairs={{0,12},{1,13},{2,14},{3,15},{4,8},{5,9},{6,10},{7,11},{8,4},{9,5},... | collective-permute-start | bytes 49160 | tf_op jit(solution)/shard_map/ppermute | solution.py:530
  6.3 0.1 collective-permute-start
  6.4 2.3 %prep.1 = (bf16[2,1280,128]{2,1,0:T(8,128)(2,1)S(1)}, bf16[16,1024]{1,0:T(8,128)(2,1)S(1)}, f32[1024,128]{1,0:T(8,128)S(1)}, f32[2,16,256]{2,1,0:T(8,128)S(1)}) custom-call(f32[2,16]{1,0:T(2,128)} %rates_hbm.1, bf16[16,1024]{1,0:T(8,128)(2,1)} %emb_hbm.1, f32[1,1024]{1,0:T(1,128)} %bitcast.2, bf16[1024,2304]{1,0:T(8,128)(2,1)} %in_hbm.3, ...), custom_call_target="tpu_custom_call" | custom-call | flops 100000000 | bytes 12000000 | tf_op jit(solution)/shard_map/prep/pallas_call | solution.py:534
  8.7 2.3 %local.1 = (bf16[2,16,256,256]{3,2,1,0:T(8,128)(2,1)S(1)}, f32[1024,256]{1,0:T(8,128)S(1)}, f32[2,16,256]{2,1,0:T(8,128)S(1)}) custom-call(s32[1,16,256]{2,1,0:T(8,128)S(1)} %pack.1.held_ref, f32[2,16,256]{2,1,0:T(8,128)S(1)} %get-tuple-element.34.rate_ref, bf16[16,1024]{1,0:T(8,128)(2,1)S(1)} %get-tuple-element.35.norm_ref, bf16[1024,2304]{1,0:T(8,128)(2,1)} %in_hbm.3), custom_call_target="tpu_custom_call" | custom-call | flops 20000000 | bytes 5000000 | tf_op jit(solution)/shard_map/local/pallas_call | solution.py:562
  11.1 0.0 collective-permute-done.2
  11.1 0.0 collective-permute-done.1
  11.1 0.0 collective-permute-done
  11.1 1.6 %collective-permute-start.3 = (s32[4,16,256]{2,1,0:T(8,128)S(1)}, s32[4,16,256]{2,1,0:T(8,128)S(1)}, u32[]{:S(2)}, u32[]{:S(2)}) collective-permute-start(s32[4,16,256]{2,1,0:T(8,128)S(1)} %pad_add_fusion.1.held_ref.near_ref), channel_id=1, source_target_pairs={{0,2},{1,3},{2,0},{3,1},{4,6},{5,7},{6,4},{7,5},{8,10},{9,11},{10,... | collective-permute-start | bytes 196616 | tf_op jit(solution)/shard_map/ppermute | solution.py:530
  12.7 0.0 copy-start
  12.7 1.4 %spans.2 = (f32[4,1024,128]{2,1,0:T(8,128)S(1)}, f32[2,4,16,256]{3,2,1,0:T(8,128)S(1)}, f32[4,16,256]{2,1,0:T(8,128)S(1)}) custom-call(s32[4,16,256]{2,1,0:T(8,128)S(1)} %pad_add_fusion.1.held_ref.near_ref, bf16[2,1280,128]{2,1,0:T(8,128)(2,1)S(1)} %get-tuple-element.40.conv_ref, f32[2,16,256]{2,1,0:T(8,128)S(1)} %get-tuple-element.34.rate_ref), custom_call_target="tpu_custom_call" | custom-call | flops 2000000000 | bytes 4000000 | tf_op jit(solution)/shard_map/spans/pallas_call | solution.py:577
  14.1 0.2 copy-done
  14.3 0.6 %turn.1.out_ref = bf16[1024,1024]{1,0:T(8,128)(2,1)S(1)} custom-call(s32[4,16,256]{2,1,0:T(8,128)S(1)} %pad_add_fusion.1.held_ref.near_ref, bf16[1024,1024]{1,0:T(8,128)(2,1)S(1)} %copy-done), custom_call_target="tpu_custom_call" | custom-call | flops 40000000 | bytes 6000000 | tf_op jit(solution)/shard_map/turn/pallas_call | solution.py:595
  14.9 0.5 %collective-permute-done.3 = s32[4,16,256]{2,1,0:T(8,128)S(1)} collective-permute-done((s32[4,16,256]{2,1,0:T(8,128)S(1)}, s32[4,16,256]{2,1,0:T(8,128)S(1)}, u32[]{:S(2)}, u32[]{:S(2)}) %collective-permute-start.3) | collective-permute-done | bytes 65568 | tf_op jit(solution)/shard_map/ppermute | solution.py:530
  15.5 0.1 collective-permute-start.4
  15.5 1.4 %spans.3 = (f32[4,1024,128]{2,1,0:T(8,128)S(1)}, f32[2,4,16,256]{3,2,1,0:T(8,128)S(1)}, f32[4,16,256]{2,1,0:T(8,128)S(1)}) custom-call(s32[8,16,256]{2,1,0:T(8,128)S(1)} %pad_add_fusion.held_ref, bf16[2,1280,128]{2,1,0:T(8,128)(2,1)S(1)} %get-tuple-element.40.conv_ref, f32[2,16,256]{2,1,0:T(8,128)S(1)} %get-tuple-element.34.rate_ref), custom_call_target="tpu_custom_call" | custom-call | flops 2000000000 | bytes 4000000 | tf_op jit(solution)/shard_map/spans/pallas_call | solution.py:577
  16.9 0.0 collective-permute-done.4.far_ref
  17.0 1.6 %combine.1 = (f32[1024,256]{1,0:T(8,128)S(1)}, bf16[1024,256]{1,0:T(8,128)(2,1)S(1)}, bf16[2,128,256]{2,1,0:T(8,128)(2,1)S(1)}) custom-call(s32[8,16,256]{2,1,0:T(8,128)S(1)} %pad_add_fusion.held_ref, s32[8,16,256]{2,1,0:T(8,128)S(1)} %collective-permute-done.4.far_ref, f32[4,1024,128]{2,1,0:T(8,128)S(1)} %get-tuple-element.45.state_a, ...), custom_call_target="tpu_custom_call" | custom-call | flops 1000000000 | bytes 8000000 | tf_op jit(solution)/shard_map/combine/pallas_call | solution.py:626
  18.6 0.6 %collective-permute-start.5 = (bf16[1024,256]{1,0:T(8,128)(2,1)S(1)}, bf16[1024,256]{1,0:T(8,128)(2,1)S(1)}, u32[]{:S(2)}, u32[]{:S(2)}) collective-permute-start(bf16[1024,256]{1,0:T(8,128)(2,1)S(1)} %get-tuple-element.52), channel_id=1, source_target_pairs={{0,1},{1,0},{2,3},{3,2},{4,5},{5,4},{6,7},{7,6},{8,9},{9,8},{10,11... | collective-permute-start | bytes 1572872 | tf_op jit(solution)/shard_map/ppermute | solution.py:530
  19.2 1.4 %own.1 = (f32[1024,256]{1,0:T(8,128)S(1)}, bf16[1024,256]{1,0:T(8,128)(2,1)S(1)}, bf16[256,256]{1,0:T(8,128)(2,1)S(1)}, bf16[2,128,256]{2,1,0:T(8,128)(2,1)S(1)}) custom-call(bf16[2,128,256]{2,1,0:T(8,128)(2,1)S(1)} %get-tuple-element.55.onehot_ref, bf16[2,1280,128]{2,1,0:T(8,128)(2,1)S(1)} %get-tuple-element.40.conv_ref, ...), custom_call_target="tpu_custom_call" | custom-call | flops 3000000000 | bytes 9000000 | tf_op jit(solution)/shard_map/own/pallas_call | solution.py:669
  20.5 0.2 collective-permute-done.5.mate_ref
  20.7 2.5 %output.1 = bf16[256,1024]{1,0:T(8,128)(2,1)} custom-call(f32[1024,256]{1,0:T(8,128)S(1)} %get-tuple-element.51.mine_ref, bf16[1024,256]{1,0:T(8,128)(2,1)S(1)} %collective-permute-done.5.mate_ref, f32[2,16,256]{2,1,0:T(8,128)S(1)} %get-tuple-element.53.reach_ref, bf16[2,16,256,256]{3,2,1,0:T(8,128)(2,1)S(1)} %get-tuple-element.54.decay_ref, ...), custom_call_target="tpu_custom_call" | custom-call | flops 2000000000 | bytes 6000000 | tf_op jit(solution)/shard_map/output/pallas_call | solution.py:683
  (2 shorter events, 0.0 us)
Async XLA Ops:
  0.8 10.3 %collective-permute-start.2 = (s32[1,16,256]{2,1,0:T(8,128)S(1)}, s32[1,16,256]{2,1,0:T(8,128)S(1)}, u32[]{:S(2)}, u32[]{:S(2)}) collective-permute-start(s32[1,16,256]{2,1,0:T(8,128)S(1)} %pack.1.held_ref), channel_id=1, source_target_pairs={{0,4},{1,5},{2,6},{3,7},{4,0},{5,1},{6,2},{7,3},{8,12},{9,13},{10,... | collective-permute-start | bytes 49160 | tf_op jit(solution)/shard_map/ppermute | solution.py:530
  3.9 7.2 %collective-permute-start.1 = (s32[1,16,256]{2,1,0:T(8,128)S(1)}, s32[1,16,256]{2,1,0:T(8,128)S(1)}, u32[]{:S(2)}, u32[]{:S(2)}) collective-permute-start(s32[1,16,256]{2,1,0:T(8,128)S(1)} %pack.1.held_ref), channel_id=1, source_target_pairs={{0,12},{1,13},{2,14},{3,15},{4,8},{5,9},{6,10},{7,11},{8,4},{9,5},... | collective-permute-start | bytes 49160 | tf_op jit(solution)/shard_map/ppermute | solution.py:530
  6.3 4.8 %collective-permute-start = (s32[1,16,256]{2,1,0:T(8,128)S(1)}, s32[1,16,256]{2,1,0:T(8,128)S(1)}, u32[]{:S(2)}, u32[]{:S(2)}) collective-permute-start(s32[1,16,256]{2,1,0:T(8,128)S(1)} %pack.1.held_ref), channel_id=1, source_target_pairs={{0,8},{1,9},{2,10},{3,11},{4,12},{5,13},{6,14},{7,15},{8,0},{9,1},... | collective-permute-start | bytes 49160 | tf_op jit(solution)/shard_map/ppermute | solution.py:530
  11.1 4.3 %collective-permute-start.3 = (s32[4,16,256]{2,1,0:T(8,128)S(1)}, s32[4,16,256]{2,1,0:T(8,128)S(1)}, u32[]{:S(2)}, u32[]{:S(2)}) collective-permute-start(s32[4,16,256]{2,1,0:T(8,128)S(1)} %pad_add_fusion.1.held_ref.near_ref), channel_id=1, source_target_pairs={{0,2},{1,3},{2,0},{3,1},{4,6},{5,7},{6,4},{7,5},{8,10},{9,11},{10,... | collective-permute-start | bytes 196616 | tf_op jit(solution)/shard_map/ppermute | solution.py:530
  12.7 1.6 %copy-start = (bf16[1024,1024]{1,0:T(8,128)(2,1)S(1)}, bf16[1024,1024]{1,0:T(8,128)(2,1)}, u32[]{:S(2)}) copy-start(bf16[1024,1024]{1,0:T(8,128)(2,1)} %out_ref.1) | copy-start | bytes 6291460
  15.5 1.5 %collective-permute-start.4 = (s32[8,16,256]{2,1,0:T(8,128)S(1)}, s32[8,16,256]{2,1,0:T(8,128)S(1)}, u32[]{:S(2)}, u32[]{:S(2)}) collective-permute-start(s32[8,16,256]{2,1,0:T(8,128)S(1)} %pad_add_fusion.held_ref), channel_id=1, source_target_pairs={{0,1},{1,0},{2,3},{3,2},{4,5},{5,4},{6,7},{7,6},{8,9},{9,8},{10,11... | collective-permute-start | bytes 393224 | tf_op jit(solution)/shard_map/ppermute | solution.py:530
  18.6 2.1 %collective-permute-start.5 = (bf16[1024,256]{1,0:T(8,128)(2,1)S(1)}, bf16[1024,256]{1,0:T(8,128)(2,1)S(1)}, u32[]{:S(2)}, u32[]{:S(2)}) collective-permute-start(bf16[1024,256]{1,0:T(8,128)(2,1)S(1)} %get-tuple-element.52), channel_id=1, source_target_pairs={{0,1},{1,0},{2,3},{3,2},{4,5},{5,4},{6,7},{7,6},{8,9},{9,8},{10,11... | collective-permute-start | bytes 1572872 | tf_op jit(solution)/shard_map/ppermute | solution.py:530

commit v4 on v3

--- a/solution.py
+++ b/solution.py
@@ -320,7 +320,7 @@
     masks,
     held_ref, far_ref, state_a, within_a, total_a, state_b, within_b, total_b, conv_ref, rate_ref,
     mine_ref, mate_ref, onehot_ref,
-    totals, between, ids, shifted,
+    totals, between, ids, shifted, sums,
 ):
     count = 2 * len(masks)
     heads, span = held_ref.shape[1:]
@@ -361,13 +361,30 @@
         one = jnp.concatenate(found, axis=0).astype(BF16)
         onehot_ref[b] = jnp.concatenate([one, one], axis=0)
 
+    scales = []
+    for slot, mask in enumerate(masks):
+        c = jnp.bitwise_xor(me, mask)
+        rev = c > me
+        scale = jnp.exp(-rate_ref[rev.astype(jnp.int32), :, :LANES] * between[c])
+        scales.append((jnp.where(rev, 0.0, scale), jnp.where(rev, scale, 0.0)))
+    for h in range(heads):
+        rows = slice(h * head, (h + 1) * head)
+        ahead = behind = None
+        for slot in range(1, len(masks)):
+            state, _, _, k = parts[slot]
+            value = state[k, rows]
+            fore, back = (value * scales[slot][i][h : h + 1] for i in range(2))
+            ahead = fore if ahead is None else ahead + fore
+            behind = back if behind is None else behind + back
+        sums[rows, :width] = ahead
+        sums[rows, width:] = behind
+
     lane = lax.broadcasted_iota(jnp.int32, (1, span), 1)
     token = jnp.full((8, span), -1, jnp.int32)
     kind = jnp.full((1, span), -1, jnp.int32)
     side = jnp.full((1, span), -1, jnp.int32)
     dist = jnp.zeros((heads, LANES), F32)
     rate = jnp.zeros((heads, LANES), F32)
-    scales = []
     for slot, mask in enumerate(masks):
         c = jnp.bitwise_xor(me, mask)
         rev = (c > me) if mask else core == 1
@@ -390,8 +407,6 @@
         gap = moved(within[1, k], within[0, k])[:, :LANES] + between[c]
         dist = jnp.where(near, gap, dist)
         rate = jnp.where(near, rate_ref[b, :, :LANES], rate)
-        scale = jnp.exp(-rate_ref[b, :, :LANES] * between[c])
-        scales.append((jnp.where(rev, 0.0, scale), jnp.where(rev, scale, 0.0)))
     values = values[:, :LANES]
     found = [jnp.where(values == token[j : j + 1, :LANES], 1.0, 0.0) for j in range(4)]
     one = jnp.concatenate(found, axis=0)
@@ -407,21 +422,14 @@
     edges = dot(x.reshape(inner, LANES).astype(BF16), bt.astype(BF16), NT)
 
     through = [jnp.exp(-rate_ref[b, :, :LANES] * totals[base + b]) for b in range(2)]
+    zero = core == 0
     for h in range(heads):
         rows = slice(h * head, (h + 1) * head)
-        ahead, behind = edges[rows, :width], edges[rows, width : 2 * width]
-        own = edges[rows, 2 * width :]
-        for slot, mask in enumerate(masks):
-            state, _, _, k = parts[slot]
-            value = state[k, rows]
-            if not mask:
-                own = own + value
-                continue
-            ahead = ahead + value * scales[slot][0][h : h + 1]
-            behind = behind + value * scales[slot][1][h : h + 1]
+        ahead = sums[rows, :width] + edges[rows, :width]
+        behind = sums[rows, width:] + edges[rows, width : 2 * width]
+        own = edges[rows, 2 * width :] + parts[0][0][0, rows]
         ahead_next = ahead * through[0][h : h + 1]
         behind_next = behind * through[1][h : h + 1]
-        zero = core == 0
         mine_ref[rows, :width] = jnp.where(zero, ahead, ahead_next)
         mine_ref[rows, width:] = jnp.where(zero, behind_next, behind)
         mate_ref[rows, :width] = jnp.where(zero, ahead_next + own, ahead).astype(BF16)
@@ -633,6 +641,7 @@
                 pltpu.VMEM((count, heads, LANES), F32),
                 pltpu.VMEM((count, span), jnp.int32),
                 pltpu.VMEM((7, count, span), jnp.int32),
+                pltpu.VMEM((inner, 2 * width), F32),
             ],
             compiler_params=pltpu.CompilerParams(vmem_limit_bytes=12 * MIB),
             name="combine",

time: 23.4 us -> 23.3 us (level)
  no operation moved by 1% of the time
where the time goes in v4:
time: 23.3 us; the launch traced here: 23 us
  Pallas kernels  14.1 us (61%)
  starting transfers between devices  7.87 us (34%)
  waiting for transfers between devices  0.73 us (3%)
    ppermute x6, starting transfers between devices, swap(): return lax.ppermute(value, 'seq', [(i, i ^ mask) for i in range(count)])  7.87 us
    pallas_call x2, Pallas kernels, spans(): pl.pallas_call(functools.partial(spans_kernel, first, some), out_shape=(f...  2.81 us
    pallas_call x1, Pallas kernels, shards(): pl.pallas_call(functools.partial(output_kernel, summed), out_shape=b16(sp...  2.5 us
    pallas_call x1, Pallas kernels, shards(): pl.pallas_call(local_kernel, out_shape=(b16(2, heads, span, span), f32(in...  2.32 us
    pallas_call x1, Pallas kernels, shards(): pl.pallas_call(prep_kernel, out_shape=(b16(2, wide, 2 * taps * vocab), b1...  2.29 us
    pallas_call x1, Pallas kernels, shards(): pl.pallas_call(functools.partial(combine_kernel, masks), out_shape=(f32(i...  1.45 us
    pallas_call x1, Pallas kernels, shards(): pl.pallas_call(own_kernel, out_shape=(f32(inner, span), b16(inner, span),...  1.35 us
    pallas_call x1, Pallas kernels, shards(): pl.pallas_call(pack_kernel, out_shape=jax.ShapeDtypeStruct((1, heads, spa...  0.75 us
  transfers between devices with their start and end apart: 6, of which 2 were waited for; matrix products, arithmetic and copies ran while one was open for 0% of the time, Pallas kernels for 41%

profile of v4, /device:TPU:0, one launch (start us, length us, event | category | flops | bytes accessed | tf_op | source)
XLA Modules:
  0.0 23.0 jit_solution(9429546934072496284)
XLA Ops:
  0.0 0.8 %pack.1.held_ref = s32[1,16,256]{2,1,0:T(8,128)S(1)} custom-call(s32[1,256]{1,0:T(1,128)} %bitcast.3, s32[16,256]{1,0:T(8,128)} %exp_ref.1), custom_call_target="tpu_custom_call" | custom-call | tf_op jit(solution)/shard_map/pack/pallas_call | solution.py:523
  0.8 3.1 %collective-permute-start.2 = (s32[1,16,256]{2,1,0:T(8,128)S(1)}, s32[1,16,256]{2,1,0:T(8,128)S(1)}, u32[]{:S(2)}, u32[]{:S(2)}) collective-permute-start(s32[1,16,256]{2,1,0:T(8,128)S(1)} %pack.1.held_ref), channel_id=1, source_target_pairs={{0,4},{1,5},{2,6},{3,7},{4,0},{5,1},{6,2},{7,3},{8,12},{9,13},{10,... | collective-permute-start | bytes 49160 | tf_op jit(solution)/shard_map/ppermute | solution.py:538
  3.9 2.5 %collective-permute-start.1 = (s32[1,16,256]{2,1,0:T(8,128)S(1)}, s32[1,16,256]{2,1,0:T(8,128)S(1)}, u32[]{:S(2)}, u32[]{:S(2)}) collective-permute-start(s32[1,16,256]{2,1,0:T(8,128)S(1)} %pack.1.held_ref), channel_id=1, source_target_pairs={{0,12},{1,13},{2,14},{3,15},{4,8},{5,9},{6,10},{7,11},{8,4},{9,5},... | collective-permute-start | bytes 49160 | tf_op jit(solution)/shard_map/ppermute | solution.py:538
  6.3 0.1 collective-permute-start
  6.4 2.3 %prep.1 = (bf16[2,1280,128]{2,1,0:T(8,128)(2,1)S(1)}, bf16[16,1024]{1,0:T(8,128)(2,1)S(1)}, f32[1024,128]{1,0:T(8,128)S(1)}, f32[2,16,256]{2,1,0:T(8,128)S(1)}) custom-call(f32[2,16]{1,0:T(2,128)} %rates_hbm.1, bf16[16,1024]{1,0:T(8,128)(2,1)} %emb_hbm.1, f32[1,1024]{1,0:T(1,128)} %bitcast.2, bf16[1024,2304]{1,0:T(8,128)(2,1)} %in_hbm.3, ...), custom_call_target="tpu_custom_call" | custom-call | flops 100000000 | bytes 12000000 | tf_op jit(solution)/shard_map/prep/pallas_call | solution.py:542
  8.7 2.3 %local.1 = (bf16[2,16,256,256]{3,2,1,0:T(8,128)(2,1)S(1)}, f32[1024,256]{1,0:T(8,128)S(1)}, f32[2,16,256]{2,1,0:T(8,128)S(1)}) custom-call(s32[1,16,256]{2,1,0:T(8,128)S(1)} %pack.1.held_ref, f32[2,16,256]{2,1,0:T(8,128)S(1)} %get-tuple-element.34.rate_ref, bf16[16,1024]{1,0:T(8,128)(2,1)S(1)} %get-tuple-element.35.norm_ref, bf16[1024,2304]{1,0:T(8,128)(2,1)} %in_hbm.3), custom_call_target="tpu_custom_call" | custom-call | flops 20000000 | bytes 5000000 | tf_op jit(solution)/shard_map/local/pallas_call | solution.py:570
  11.1 0.0 collective-permute-done.2
  11.1 0.0 collective-permute-done.1
  11.1 0.0 collective-permute-done
  11.1 1.6 %collective-permute-start.3 = (s32[4,16,256]{2,1,0:T(8,128)S(1)}, s32[4,16,256]{2,1,0:T(8,128)S(1)}, u32[]{:S(2)}, u32[]{:S(2)}) collective-permute-start(s32[4,16,256]{2,1,0:T(8,128)S(1)} %pad_add_fusion.1.held_ref.near_ref), channel_id=1, source_target_pairs={{0,2},{1,3},{2,0},{3,1},{4,6},{5,7},{6,4},{7,5},{8,10},{9,11},{10,... | collective-permute-start | bytes 196616 | tf_op jit(solution)/shard_map/ppermute | solution.py:538
  12.7 0.0 copy-start
  12.7 1.4 %spans.2 = (f32[4,1024,128]{2,1,0:T(8,128)S(1)}, f32[2,4,16,256]{3,2,1,0:T(8,128)S(1)}, f32[4,16,256]{2,1,0:T(8,128)S(1)}) custom-call(s32[4,16,256]{2,1,0:T(8,128)S(1)} %pad_add_fusion.1.held_ref.near_ref, bf16[2,1280,128]{2,1,0:T(8,128)(2,1)S(1)} %get-tuple-element.40.conv_ref, f32[2,16,256]{2,1,0:T(8,128)S(1)} %get-tuple-element.34.rate_ref), custom_call_target="tpu_custom_call" | custom-call | flops 2000000000 | bytes 4000000 | tf_op jit(solution)/shard_map/spans/pallas_call | solution.py:585
  14.1 0.2 copy-done
  14.3 0.6 %turn.1.out_ref = bf16[1024,1024]{1,0:T(8,128)(2,1)S(1)} custom-call(s32[4,16,256]{2,1,0:T(8,128)S(1)} %pad_add_fusion.1.held_ref.near_ref, bf16[1024,1024]{1,0:T(8,128)(2,1)S(1)} %copy-done), custom_call_target="tpu_custom_call" | custom-call | flops 40000000 | bytes 6000000 | tf_op jit(solution)/shard_map/turn/pallas_call | solution.py:603
  14.9 0.5 %collective-permute-done.3 = s32[4,16,256]{2,1,0:T(8,128)S(1)} collective-permute-done((s32[4,16,256]{2,1,0:T(8,128)S(1)}, s32[4,16,256]{2,1,0:T(8,128)S(1)}, u32[]{:S(2)}, u32[]{:S(2)}) %collective-permute-start.3) | collective-permute-done | bytes 65568 | tf_op jit(solution)/shard_map/ppermute | solution.py:538
  15.5 0.1 collective-permute-start.4
  15.5 1.4 %spans.3 = (f32[4,1024,128]{2,1,0:T(8,128)S(1)}, f32[2,4,16,256]{3,2,1,0:T(8,128)S(1)}, f32[4,16,256]{2,1,0:T(8,128)S(1)}) custom-call(s32[8,16,256]{2,1,0:T(8,128)S(1)} %pad_add_fusion.held_ref, bf16[2,1280,128]{2,1,0:T(8,128)(2,1)S(1)} %get-tuple-element.40.conv_ref, f32[2,16,256]{2,1,0:T(8,128)S(1)} %get-tuple-element.34.rate_ref), custom_call_target="tpu_custom_call" | custom-call | flops 2000000000 | bytes 4000000 | tf_op jit(solution)/shard_map/spans/pallas_call | solution.py:585
  16.9 0.0 collective-permute-done.4.far_ref
  17.0 1.4 %combine.1 = (f32[1024,256]{1,0:T(8,128)S(1)}, bf16[1024,256]{1,0:T(8,128)(2,1)S(1)}, bf16[2,128,256]{2,1,0:T(8,128)(2,1)S(1)}) custom-call(s32[8,16,256]{2,1,0:T(8,128)S(1)} %pad_add_fusion.held_ref, s32[8,16,256]{2,1,0:T(8,128)S(1)} %collective-permute-done.4.far_ref, f32[4,1024,128]{2,1,0:T(8,128)S(1)} %get-tuple-element.45.state_a, ...), custom_call_target="tpu_custom_call" | custom-call | flops 1000000000 | bytes 8000000 | tf_op jit(solution)/shard_map/combine/pallas_call | solution.py:634
  18.4 0.6 %collective-permute-start.5 = (bf16[1024,256]{1,0:T(8,128)(2,1)S(1)}, bf16[1024,256]{1,0:T(8,128)(2,1)S(1)}, u32[]{:S(2)}, u32[]{:S(2)}) collective-permute-start(bf16[1024,256]{1,0:T(8,128)(2,1)S(1)} %get-tuple-element.52), channel_id=1, source_target_pairs={{0,1},{1,0},{2,3},{3,2},{4,5},{5,4},{6,7},{7,6},{8,9},{9,8},{10,11... | collective-permute-start | bytes 1572872 | tf_op jit(solution)/shard_map/ppermute | solution.py:538
  19.0 1.4 %own.1 = (f32[1024,256]{1,0:T(8,128)S(1)}, bf16[1024,256]{1,0:T(8,128)(2,1)S(1)}, bf16[256,256]{1,0:T(8,128)(2,1)S(1)}, bf16[2,128,256]{2,1,0:T(8,128)(2,1)S(1)}) custom-call(bf16[2,128,256]{2,1,0:T(8,128)(2,1)S(1)} %get-tuple-element.55.onehot_ref, bf16[2,1280,128]{2,1,0:T(8,128)(2,1)S(1)} %get-tuple-element.40.conv_ref, ...), custom_call_target="tpu_custom_call" | custom-call | flops 3000000000 | bytes 9000000 | tf_op jit(solution)/shard_map/own/pallas_call | solution.py:678
  20.3 0.2 collective-permute-done.5.mate_ref
  20.5 2.5 %output.1 = bf16[256,1024]{1,0:T(8,128)(2,1)} custom-call(f32[1024,256]{1,0:T(8,128)S(1)} %get-tuple-element.51.mine_ref, bf16[1024,256]{1,0:T(8,128)(2,1)S(1)} %collective-permute-done.5.mate_ref, f32[2,16,256]{2,1,0:T(8,128)S(1)} %get-tuple-element.53.reach_ref, bf16[2,16,256,256]{3,2,1,0:T(8,128)(2,1)S(1)} %get-tuple-element.54.decay_ref, ...), custom_call_target="tpu_custom_call" | custom-call | flops 2000000000 | bytes 6000000 | tf_op jit(solution)/shard_map/output/pallas_call | solution.py:692
  (2 shorter events, 0.0 us)
Async XLA Ops:
  0.8 10.3 %collective-permute-start.2 = (s32[1,16,256]{2,1,0:T(8,128)S(1)}, s32[1,16,256]{2,1,0:T(8,128)S(1)}, u32[]{:S(2)}, u32[]{:S(2)}) collective-permute-start(s32[1,16,256]{2,1,0:T(8,128)S(1)} %pack.1.held_ref), channel_id=1, source_target_pairs={{0,4},{1,5},{2,6},{3,7},{4,0},{5,1},{6,2},{7,3},{8,12},{9,13},{10,... | collective-permute-start | bytes 49160 | tf_op jit(solution)/shard_map/ppermute | solution.py:538
  3.9 7.2 %collective-permute-start.1 = (s32[1,16,256]{2,1,0:T(8,128)S(1)}, s32[1,16,256]{2,1,0:T(8,128)S(1)}, u32[]{:S(2)}, u32[]{:S(2)}) collective-permute-start(s32[1,16,256]{2,1,0:T(8,128)S(1)} %pack.1.held_ref), channel_id=1, source_target_pairs={{0,12},{1,13},{2,14},{3,15},{4,8},{5,9},{6,10},{7,11},{8,4},{9,5},... | collective-permute-start | bytes 49160 | tf_op jit(solution)/shard_map/ppermute | solution.py:538
  6.3 4.8 %collective-permute-start = (s32[1,16,256]{2,1,0:T(8,128)S(1)}, s32[1,16,256]{2,1,0:T(8,128)S(1)}, u32[]{:S(2)}, u32[]{:S(2)}) collective-permute-start(s32[1,16,256]{2,1,0:T(8,128)S(1)} %pack.1.held_ref), channel_id=1, source_target_pairs={{0,8},{1,9},{2,10},{3,11},{4,12},{5,13},{6,14},{7,15},{8,0},{9,1},... | collective-permute-start | bytes 49160 | tf_op jit(solution)/shard_map/ppermute | solution.py:538
  11.1 4.3 %collective-permute-start.3 = (s32[4,16,256]{2,1,0:T(8,128)S(1)}, s32[4,16,256]{2,1,0:T(8,128)S(1)}, u32[]{:S(2)}, u32[]{:S(2)}) collective-permute-start(s32[4,16,256]{2,1,0:T(8,128)S(1)} %pad_add_fusion.1.held_ref.near_ref), channel_id=1, source_target_pairs={{0,2},{1,3},{2,0},{3,1},{4,6},{5,7},{6,4},{7,5},{8,10},{9,11},{10,... | collective-permute-start | bytes 196616 | tf_op jit(solution)/shard_map/ppermute | solution.py:538
  12.7 1.6 %copy-start = (bf16[1024,1024]{1,0:T(8,128)(2,1)S(1)}, bf16[1024,1024]{1,0:T(8,128)(2,1)}, u32[]{:S(2)}) copy-start(bf16[1024,1024]{1,0:T(8,128)(2,1)} %out_ref.1) | copy-start | bytes 6291460
  15.5 1.5 %collective-permute-start.4 = (s32[8,16,256]{2,1,0:T(8,128)S(1)}, s32[8,16,256]{2,1,0:T(8,128)S(1)}, u32[]{:S(2)}, u32[]{:S(2)}) collective-permute-start(s32[8,16,256]{2,1,0:T(8,128)S(1)} %pad_add_fusion.held_ref), channel_id=1, source_target_pairs={{0,1},{1,0},{2,3},{3,2},{4,5},{5,4},{6,7},{7,6},{8,9},{9,8},{10,11... | collective-permute-start | bytes 393224 | tf_op jit(solution)/shard_map/ppermute | solution.py:538
  18.4 2.1 %collective-permute-start.5 = (bf16[1024,256]{1,0:T(8,128)(2,1)S(1)}, bf16[1024,256]{1,0:T(8,128)(2,1)S(1)}, u32[]{:S(2)}, u32[]{:S(2)}) collective-permute-start(bf16[1024,256]{1,0:T(8,128)(2,1)S(1)} %get-tuple-element.52), channel_id=1, source_target_pairs={{0,1},{1,0},{2,3},{3,2},{4,5},{5,4},{6,7},{7,6},{8,9},{9,8},{10,11... | collective-permute-start | bytes 1572872 | tf_op jit(solution)/shard_map/ppermute | solution.py:538

commit v5 on v4

--- a/solution.py
+++ b/solution.py
@@ -534,6 +534,22 @@
         name="pack",
     )(pin(ids[None, :]), pin(exponents))
 
+    def narrow(value):
+        many = value.shape[0]
+        low = value & 0xFFFF
+        pairs = low[:, : heads // 2] | (low[:, heads // 2 :] << 16)
+        token = value[:, 0] >> 16
+        token = token[: many // 2] | (token[many // 2 :] << 16)
+        token = jnp.pad(token, ((0, heads // 2 - many // 2), (0, 0)))
+        return jnp.concatenate([pairs, token[None]], axis=0)
+
+    def widen(value):
+        many = value.shape[0] - 1
+        pairs, token = value[:many], value[many, : many // 2]
+        both = jnp.concatenate([pairs & 0xFFFF, (pairs >> 16) & 0xFFFF], axis=1)
+        token = jnp.concatenate([token & 0xFFFF, token >> 16], axis=0)
+        return both | (token << 16)[:, None, :]
+
     def swap(value, mask):
         return lax.ppermute(value, "seq", [(i, i ^ mask) for i in range(count)])
 
@@ -617,7 +633,10 @@
     for k, stage in enumerate(stages[:-1]):
         if k == 1:
             held, local = lax.optimization_barrier((held, local))
-        new = [swap(held, mask) for mask in stage]
+        if k == 1 and summed:
+            new = [widen(swap(narrow(held), stage[0]))]
+        else:
+            new = [swap(held, mask) for mask in stage]
         if k == 1:
             turned = turn(held)
             if summed:

time: 23.3 us -> 23.3 us (level)
  waiting for transfers between devices: 0.73 us -> 0.47 us
    ppermute x6, waiting for transfers between devices: 0.73 us -> 0.47 us  [swap(): return lax.ppermute(value, 'seq', [(i, i ^ mask) for i in range(count)])]
where the time goes in v5:
time: 23.3 us; the launch traced here: 23 us
  Pallas kernels  14.1 us (61%)
  starting transfers between devices  7.87 us (34%)
  waiting for transfers between devices  0.47 us (2%)
    ppermute x6, starting transfers between devices, swap(): return lax.ppermute(value, 'seq', [(i, i ^ mask) for i in range(count)])  7.87 us
    pallas_call x2, Pallas kernels, spans(): pl.pallas_call(functools.partial(spans_kernel, first, some), out_shape=(f...  2.81 us
    pallas_call x1, Pallas kernels, shards(): pl.pallas_call(functools.partial(output_kernel, summed), out_shape=b16(sp...  2.49 us
    pallas_call x1, Pallas kernels, shards(): pl.pallas_call(local_kernel, out_shape=(b16(2, heads, span, span), f32(in...  2.32 us
    pallas_call x1, Pallas kernels, shards(): pl.pallas_call(prep_kernel, out_shape=(b16(2, wide, 2 * taps * vocab), b1...  2.29 us
    pallas_call x1, Pallas kernels, shards(): pl.pallas_call(functools.partial(combine_kernel, masks), out_shape=(f32(i...  1.44 us
    pallas_call x1, Pallas kernels, shards(): pl.pallas_call(own_kernel, out_shape=(f32(inner, span), b16(inner, span),...  1.35 us
    pallas_call x1, Pallas kernels, shards(): pl.pallas_call(pack_kernel, out_shape=jax.ShapeDtypeStruct((1, heads, spa...  0.75 us
  transfers between devices with their start and end apart: 6, of which 2 were waited for; matrix products, arithmetic and copies ran while one was open for 0% of the time, Pallas kernels for 41%

profile of v5, /device:TPU:0, one launch (start us, length us, event | category | flops | bytes accessed | tf_op | source)
XLA Modules:
  0.0 23.0 jit_solution(11754901263097672299)
XLA Ops:
  0.0 0.8 %pack.1.held_ref = s32[1,16,256]{2,1,0:T(8,128)S(1)} custom-call(s32[1,256]{1,0:T(1,128)} %bitcast.11, s32[16,256]{1,0:T(8,128)} %exp_ref.1), custom_call_target="tpu_custom_call" | custom-call | tf_op jit(solution)/shard_map/pack/pallas_call | solution.py:523
  0.8 3.1 %collective-permute-start.2 = (s32[1,16,256]{2,0,1:T(1,128)S(1)}, s32[1,16,256]{2,0,1:T(1,128)S(1)}, u32[]{:S(2)}, u32[]{:S(2)}) collective-permute-start(s32[1,16,256]{2,0,1:T(1,128)S(1)} %copy.14), channel_id=1, source_target_pairs={{0,4},{1,5},{2,6},{3,7},{4,0},{5,1},{6,2},{7,3},{8,12},{9,13},{10,... | collective-permute-start | bytes 49160 | tf_op jit(solution)/shard_map/ppermute | solution.py:554
  3.9 2.5 %collective-permute-start.1 = (s32[1,16,256]{2,0,1:T(1,128)S(1)}, s32[1,16,256]{2,0,1:T(1,128)S(1)}, u32[]{:S(2)}, u32[]{:S(2)}) collective-permute-start(s32[1,16,256]{2,0,1:T(1,128)S(1)} %copy.14), channel_id=1, source_target_pairs={{0,12},{1,13},{2,14},{3,15},{4,8},{5,9},{6,10},{7,11},{8,4},{9,5},... | collective-permute-start | bytes 49160 | tf_op jit(solution)/shard_map/ppermute | solution.py:554
  6.4 0.1 collective-permute-start
  6.5 2.3 %prep.1 = (bf16[2,1280,128]{2,1,0:T(8,128)(2,1)S(1)}, bf16[16,1024]{1,0:T(8,128)(2,1)S(1)}, f32[1024,128]{1,0:T(8,128)S(1)}, f32[2,16,256]{2,1,0:T(8,128)S(1)}) custom-call(f32[2,16]{1,0:T(2,128)} %rates_hbm.1, bf16[16,1024]{1,0:T(8,128)(2,1)} %emb_hbm.1, f32[1,1024]{1,0:T(1,128)} %bitcast.10, bf16[1024,2304]{1,0:T(8,128)(2,1)} %in_hbm.3, ...), custom_call_target="tpu_custom_call" | custom-call | flops 100000000 | bytes 12000000 | tf_op jit(solution)/shard_map/prep/pallas_call | solution.py:558
  8.8 2.3 %local.1 = (bf16[2,16,256,256]{3,2,1,0:T(8,128)(2,1)S(1)}, f32[1024,256]{1,0:T(8,128)S(1)}, f32[2,16,256]{2,1,0:T(8,128)S(1)}) custom-call(s32[1,16,256]{2,1,0:T(8,128)S(1)} %pack.1.held_ref, f32[2,16,256]{2,1,0:T(8,128)S(1)} %get-tuple-element.34.rate_ref, bf16[16,1024]{1,0:T(8,128)(2,1)S(1)} %get-tuple-element.35.norm_ref, bf16[1024,2304]{1,0:T(8,128)(2,1)} %in_hbm.3), custom_call_target="tpu_custom_call" | custom-call | flops 20000000 | bytes 5000000 | tf_op jit(solution)/shard_map/local/pallas_call | solution.py:586
  11.1 0.0 collective-permute-done.2
  11.1 0.0 collective-permute-done.1
  11.1 0.0 collective-permute-done
  11.1 0.1 pad_add_fusion.1
  11.3 1.6 %collective-permute-start.3 = (s32[5,8,256]{2,1,0:T(8,128)S(1)}, s32[5,8,256]{2,1,0:T(8,128)S(1)}, u32[]{:S(2)}, u32[]{:S(2)}) collective-permute-start(s32[5,8,256]{2,1,0:T(8,128)S(1)} %pad_add_fusion.2), channel_id=1, source_target_pairs={{0,2},{1,3},{2,0},{3,1},{4,6},{5,7},{6,4},{7,5},{8,10},{9,11},{10,... | collective-permute-start | bytes 122888 | tf_op jit(solution)/shard_map/ppermute | solution.py:554
  12.9 0.0 copy-start
  12.9 1.4 %spans.2 = (f32[4,1024,128]{2,1,0:T(8,128)S(1)}, f32[2,4,16,256]{3,2,1,0:T(8,128)S(1)}, f32[4,16,256]{2,1,0:T(8,128)S(1)}) custom-call(s32[4,16,256]{2,1,0:T(8,128)S(1)} %copy.17.held_ref.near_ref, bf16[2,1280,128]{2,1,0:T(8,128)(2,1)S(1)} %get-tuple-element.40.conv_ref, f32[2,16,256]{2,1,0:T(8,128)S(1)} %get-tuple-element.34.rate_ref), custom_call_target="tpu_custom_call" | custom-call | flops 2000000000 | bytes 4000000 | tf_op jit(solution)/shard_map/spans/pallas_call | solution.py:601
  14.3 0.2 copy-done
  14.5 0.6 %turn.1.out_ref = bf16[1024,1024]{1,0:T(8,128)(2,1)S(1)} custom-call(s32[4,16,256]{2,1,0:T(8,128)S(1)} %copy.17.held_ref.near_ref, bf16[1024,1024]{1,0:T(8,128)(2,1)S(1)} %copy-done), custom_call_target="tpu_custom_call" | custom-call | flops 40000000 | bytes 6000000 | tf_op jit(solution)/shard_map/turn/pallas_call | solution.py:619
  15.1 0.3 %collective-permute-done.3 = s32[5,8,256]{2,1,0:T(8,128)S(1)} collective-permute-done((s32[5,8,256]{2,1,0:T(8,128)S(1)}, s32[5,8,256]{2,1,0:T(8,128)S(1)}, u32[]{:S(2)}, u32[]{:S(2)}) %collective-permute-start.3) | collective-permute-done | bytes 40992 | tf_op jit(solution)/shard_map/ppermute | solution.py:554
  15.5 0.1 collective-permute-start.4
  15.5 1.4 %spans.3 = (f32[4,1024,128]{2,1,0:T(8,128)S(1)}, f32[2,4,16,256]{3,2,1,0:T(8,128)S(1)}, f32[4,16,256]{2,1,0:T(8,128)S(1)}) custom-call(s32[8,16,256]{2,1,0:T(8,128)S(1)} %pad_add_fusion.held_ref, bf16[2,1280,128]{2,1,0:T(8,128)(2,1)S(1)} %get-tuple-element.40.conv_ref, f32[2,16,256]{2,1,0:T(8,128)S(1)} %get-tuple-element.34.rate_ref), custom_call_target="tpu_custom_call" | custom-call | flops 2000000000 | bytes 4000000 | tf_op jit(solution)/shard_map/spans/pallas_call | solution.py:601
  17.0 0.0 collective-permute-done.4.far_ref
  17.0 1.4 %combine.1 = (f32[1024,256]{1,0:T(8,128)S(1)}, bf16[1024,256]{1,0:T(8,128)(2,1)S(1)}, bf16[2,128,256]{2,1,0:T(8,128)(2,1)S(1)}) custom-call(s32[8,16,256]{2,1,0:T(8,128)S(1)} %pad_add_fusion.held_ref, s32[8,16,256]{2,1,0:T(8,128)S(1)} %collective-permute-done.4.far_ref, f32[4,1024,128]{2,1,0:T(8,128)S(1)} %get-tuple-element.45.state_a, ...), custom_call_target="tpu_custom_call" | custom-call | flops 1000000000 | bytes 8000000 | tf_op jit(solution)/shard_map/combine/pallas_call | solution.py:653
  18.4 0.6 %collective-permute-start.5 = (bf16[1024,256]{1,0:T(8,128)(2,1)S(1)}, bf16[1024,256]{1,0:T(8,128)(2,1)S(1)}, u32[]{:S(2)}, u32[]{:S(2)}) collective-permute-start(bf16[1024,256]{1,0:T(8,128)(2,1)S(1)} %get-tuple-element.52), channel_id=1, source_target_pairs={{0,1},{1,0},{2,3},{3,2},{4,5},{5,4},{6,7},{7,6},{8,9},{9,8},{10,11... | collective-permute-start | bytes 1572872 | tf_op jit(solution)/shard_map/ppermute | solution.py:554
  19.0 1.4 %own.1 = (f32[1024,256]{1,0:T(8,128)S(1)}, bf16[1024,256]{1,0:T(8,128)(2,1)S(1)}, bf16[256,256]{1,0:T(8,128)(2,1)S(1)}, bf16[2,128,256]{2,1,0:T(8,128)(2,1)S(1)}) custom-call(bf16[2,128,256]{2,1,0:T(8,128)(2,1)S(1)} %get-tuple-element.55.onehot_ref, bf16[2,1280,128]{2,1,0:T(8,128)(2,1)S(1)} %get-tuple-element.40.conv_ref, ...), custom_call_target="tpu_custom_call" | custom-call | flops 3000000000 | bytes 9000000 | tf_op jit(solution)/shard_map/own/pallas_call | solution.py:697
  20.3 0.2 collective-permute-done.5.mate_ref
  20.5 2.5 %output.1 = bf16[256,1024]{1,0:T(8,128)(2,1)} custom-call(f32[1024,256]{1,0:T(8,128)S(1)} %get-tuple-element.51.mine_ref, bf16[1024,256]{1,0:T(8,128)(2,1)S(1)} %collective-permute-done.5.mate_ref, f32[2,16,256]{2,1,0:T(8,128)S(1)} %get-tuple-element.53.reach_ref, bf16[2,16,256,256]{3,2,1,0:T(8,128)(2,1)S(1)} %get-tuple-element.54.decay_ref, ...), custom_call_target="tpu_custom_call" | custom-call | flops 2000000000 | bytes 6000000 | tf_op jit(solution)/shard_map/output/pallas_call | solution.py:711
  (14 shorter events, 0.1 us)
Async XLA Ops:
  0.8 10.3 %collective-permute-start.2 = (s32[1,16,256]{2,0,1:T(1,128)S(1)}, s32[1,16,256]{2,0,1:T(1,128)S(1)}, u32[]{:S(2)}, u32[]{:S(2)}) collective-permute-start(s32[1,16,256]{2,0,1:T(1,128)S(1)} %copy.14), channel_id=1, source_target_pairs={{0,4},{1,5},{2,6},{3,7},{4,0},{5,1},{6,2},{7,3},{8,12},{9,13},{10,... | collective-permute-start | bytes 49160 | tf_op jit(solution)/shard_map/ppermute | solution.py:554
  3.9 7.2 %collective-permute-start.1 = (s32[1,16,256]{2,0,1:T(1,128)S(1)}, s32[1,16,256]{2,0,1:T(1,128)S(1)}, u32[]{:S(2)}, u32[]{:S(2)}) collective-permute-start(s32[1,16,256]{2,0,1:T(1,128)S(1)} %copy.14), channel_id=1, source_target_pairs={{0,12},{1,13},{2,14},{3,15},{4,8},{5,9},{6,10},{7,11},{8,4},{9,5},... | collective-permute-start | bytes 49160 | tf_op jit(solution)/shard_map/ppermute | solution.py:554
  6.4 4.8 %collective-permute-start = (s32[1,16,256]{2,0,1:T(1,128)S(1)}, s32[1,16,256]{2,0,1:T(1,128)S(1)}, u32[]{:S(2)}, u32[]{:S(2)}) collective-permute-start(s32[1,16,256]{2,0,1:T(1,128)S(1)} %copy.14), channel_id=1, source_target_pairs={{0,8},{1,9},{2,10},{3,11},{4,12},{5,13},{6,14},{7,15},{8,0},{9,1},... | collective-permute-start | bytes 49160 | tf_op jit(solution)/shard_map/ppermute | solution.py:554
  11.3 4.1 %collective-permute-start.3 = (s32[5,8,256]{2,1,0:T(8,128)S(1)}, s32[5,8,256]{2,1,0:T(8,128)S(1)}, u32[]{:S(2)}, u32[]{:S(2)}) collective-permute-start(s32[5,8,256]{2,1,0:T(8,128)S(1)} %pad_add_fusion.2), channel_id=1, source_target_pairs={{0,2},{1,3},{2,0},{3,1},{4,6},{5,7},{6,4},{7,5},{8,10},{9,11},{10,... | collective-permute-start | bytes 122888 | tf_op jit(solution)/shard_map/ppermute | solution.py:554
  12.9 1.6 %copy-start = (bf16[1024,1024]{1,0:T(8,128)(2,1)S(1)}, bf16[1024,1024]{1,0:T(8,128)(2,1)}, u32[]{:S(2)}) copy-start(bf16[1024,1024]{1,0:T(8,128)(2,1)} %out_ref.1) | copy-start | bytes 6291460
  15.5 1.5 %collective-permute-start.4 = (s32[8,16,256]{2,1,0:T(8,128)S(1)}, s32[8,16,256]{2,1,0:T(8,128)S(1)}, u32[]{:S(2)}, u32[]{:S(2)}) collective-permute-start(s32[8,16,256]{2,1,0:T(8,128)S(1)} %pad_add_fusion.held_ref), channel_id=1, source_target_pairs={{0,1},{1,0},{2,3},{3,2},{4,5},{5,4},{6,7},{7,6},{8,9},{9,8},{10,11... | collective-permute-start | bytes 393224 | tf_op jit(solution)/shard_map/ppermute | solution.py:554
  18.4 2.1 %collective-permute-start.5 = (bf16[1024,256]{1,0:T(8,128)(2,1)S(1)}, bf16[1024,256]{1,0:T(8,128)(2,1)S(1)}, u32[]{:S(2)}, u32[]{:S(2)}) collective-permute-start(bf16[1024,256]{1,0:T(8,128)(2,1)S(1)} %get-tuple-element.52), channel_id=1, source_target_pairs={{0,1},{1,0},{2,3},{3,2},{4,5},{5,4},{6,7},{7,6},{8,9},{9,8},{10,11... | collective-permute-start | bytes 1572872 | tf_op jit(solution)/shard_map/ppermute | solution.py:554

commit v6 on v5

--- a/solution.py
+++ b/solution.py
@@ -366,16 +366,20 @@
         c = jnp.bitwise_xor(me, mask)
         rev = c > me
         scale = jnp.exp(-rate_ref[rev.astype(jnp.int32), :, :LANES] * between[c])
-        scales.append((jnp.where(rev, 0.0, scale), jnp.where(rev, scale, 0.0)))
+        scales.append(scale)
     for h in range(heads):
         rows = slice(h * head, (h + 1) * head)
-        ahead = behind = None
+        groups = {}
         for slot in range(1, len(masks)):
             state, _, _, k = parts[slot]
-            value = state[k, rows]
-            fore, back = (value * scales[slot][i][h : h + 1] for i in range(2))
-            ahead = fore if ahead is None else ahead + fore
-            behind = back if behind is None else behind + back
+            value = state[k, rows] * scales[slot][h : h + 1]
+            top = 1 << (masks[slot].bit_length() - 1)
+            groups[top] = groups[top] + value if top in groups else value
+        ahead = behind = 0.0
+        for top, value in groups.items():
+            rev = (me & top) == 0
+            ahead = ahead + jnp.where(rev, 0.0, value)
+            behind = behind + jnp.where(rev, value, 0.0)
         sums[rows, :width] = ahead
         sums[rows, width:] = behind
 

time: 23.3 us -> 23.2 us (level)
  no operation moved by 1% of the time
where the time goes in v6:
time: 23.2 us; the launch traced here: 22.9 us
  Pallas kernels  14 us (60%)
  starting transfers between devices  7.87 us (34%)
  waiting for transfers between devices  0.46 us (2%)
    ppermute x6, starting transfers between devices, swap(): return lax.ppermute(value, 'seq', [(i, i ^ mask) for i in range(count)])  7.87 us
    pallas_call x2, Pallas kernels, spans(): pl.pallas_call(functools.partial(spans_kernel, first, some), out_shape=(f...  2.81 us
    pallas_call x1, Pallas kernels, shards(): pl.pallas_call(functools.partial(output_kernel, summed), out_shape=b16(sp...  2.49 us
    pallas_call x1, Pallas kernels, shards(): pl.pallas_call(local_kernel, out_shape=(b16(2, heads, span, span), f32(in...  2.32 us
    pallas_call x1, Pallas kernels, shards(): pl.pallas_call(prep_kernel, out_shape=(b16(2, wide, 2 * taps * vocab), b1...  2.29 us
    pallas_call x1, Pallas kernels, shards(): pl.pallas_call(own_kernel, out_shape=(f32(inner, span), b16(inner, span),...  1.36 us
    pallas_call x1, Pallas kernels, shards(): pl.pallas_call(functools.partial(combine_kernel, masks), out_shape=(f32(i...  1.34 us
    pallas_call x1, Pallas kernels, shards(): pl.pallas_call(pack_kernel, out_shape=jax.ShapeDtypeStruct((1, heads, spa...  0.75 us
  transfers between devices with their start and end apart: 6, of which 2 were waited for; matrix products, arithmetic and copies ran while one was open for 0% of the time, Pallas kernels for 41%

profile of v6, /device:TPU:0, one launch (start us, length us, event | category | flops | bytes accessed | tf_op | source)
XLA Modules:
  0.0 22.9 jit_solution(17315909873470776543)
XLA Ops:
  0.0 0.8 %pack.1.held_ref = s32[1,16,256]{2,1,0:T(8,128)S(1)} custom-call(s32[1,256]{1,0:T(1,128)} %bitcast.11, s32[16,256]{1,0:T(8,128)} %exp_ref.1), custom_call_target="tpu_custom_call" | custom-call | tf_op jit(solution)/shard_map/pack/pallas_call | solution.py:527
  0.8 3.1 %collective-permute-start.2 = (s32[1,16,256]{2,0,1:T(1,128)S(1)}, s32[1,16,256]{2,0,1:T(1,128)S(1)}, u32[]{:S(2)}, u32[]{:S(2)}) collective-permute-start(s32[1,16,256]{2,0,1:T(1,128)S(1)} %copy.14), channel_id=1, source_target_pairs={{0,4},{1,5},{2,6},{3,7},{4,0},{5,1},{6,2},{7,3},{8,12},{9,13},{10,... | collective-permute-start | bytes 49160 | tf_op jit(solution)/shard_map/ppermute | solution.py:558
  3.9 2.5 %collective-permute-start.1 = (s32[1,16,256]{2,0,1:T(1,128)S(1)}, s32[1,16,256]{2,0,1:T(1,128)S(1)}, u32[]{:S(2)}, u32[]{:S(2)}) collective-permute-start(s32[1,16,256]{2,0,1:T(1,128)S(1)} %copy.14), channel_id=1, source_target_pairs={{0,12},{1,13},{2,14},{3,15},{4,8},{5,9},{6,10},{7,11},{8,4},{9,5},... | collective-permute-start | bytes 49160 | tf_op jit(solution)/shard_map/ppermute | solution.py:558
  6.4 0.1 collective-permute-start
  6.5 2.3 %prep.1 = (bf16[2,1280,128]{2,1,0:T(8,128)(2,1)S(1)}, bf16[16,1024]{1,0:T(8,128)(2,1)S(1)}, f32[1024,128]{1,0:T(8,128)S(1)}, f32[2,16,256]{2,1,0:T(8,128)S(1)}) custom-call(f32[2,16]{1,0:T(2,128)} %rates_hbm.1, bf16[16,1024]{1,0:T(8,128)(2,1)} %emb_hbm.1, f32[1,1024]{1,0:T(1,128)} %bitcast.10, bf16[1024,2304]{1,0:T(8,128)(2,1)} %in_hbm.3, ...), custom_call_target="tpu_custom_call" | custom-call | flops 100000000 | bytes 12000000 | tf_op jit(solution)/shard_map/prep/pallas_call | solution.py:562
  8.8 2.3 %local.1 = (bf16[2,16,256,256]{3,2,1,0:T(8,128)(2,1)S(1)}, f32[1024,256]{1,0:T(8,128)S(1)}, f32[2,16,256]{2,1,0:T(8,128)S(1)}) custom-call(s32[1,16,256]{2,1,0:T(8,128)S(1)} %pack.1.held_ref, f32[2,16,256]{2,1,0:T(8,128)S(1)} %get-tuple-element.34.rate_ref, bf16[16,1024]{1,0:T(8,128)(2,1)S(1)} %get-tuple-element.35.norm_ref, bf16[1024,2304]{1,0:T(8,128)(2,1)} %in_hbm.3), custom_call_target="tpu_custom_call" | custom-call | flops 20000000 | bytes 5000000 | tf_op jit(solution)/shard_map/local/pallas_call | solution.py:590
  11.1 0.0 collective-permute-done.2
  11.1 0.0 collective-permute-done.1
  11.1 0.0 collective-permute-done
  11.1 0.1 pad_add_fusion.1
  11.3 1.6 %collective-permute-start.3 = (s32[5,8,256]{2,1,0:T(8,128)S(1)}, s32[5,8,256]{2,1,0:T(8,128)S(1)}, u32[]{:S(2)}, u32[]{:S(2)}) collective-permute-start(s32[5,8,256]{2,1,0:T(8,128)S(1)} %pad_add_fusion.2), channel_id=1, source_target_pairs={{0,2},{1,3},{2,0},{3,1},{4,6},{5,7},{6,4},{7,5},{8,10},{9,11},{10,... | collective-permute-start | bytes 122888 | tf_op jit(solution)/shard_map/ppermute | solution.py:558
  12.9 0.0 copy-start
  12.9 1.4 %spans.2 = (f32[4,1024,128]{2,1,0:T(8,128)S(1)}, f32[2,4,16,256]{3,2,1,0:T(8,128)S(1)}, f32[4,16,256]{2,1,0:T(8,128)S(1)}) custom-call(s32[4,16,256]{2,1,0:T(8,128)S(1)} %copy.17.held_ref.near_ref, bf16[2,1280,128]{2,1,0:T(8,128)(2,1)S(1)} %get-tuple-element.40.conv_ref, f32[2,16,256]{2,1,0:T(8,128)S(1)} %get-tuple-element.34.rate_ref), custom_call_target="tpu_custom_call" | custom-call | flops 2000000000 | bytes 4000000 | tf_op jit(solution)/shard_map/spans/pallas_call | solution.py:605
  14.3 0.2 copy-done
  14.5 0.6 %turn.1.out_ref = bf16[1024,1024]{1,0:T(8,128)(2,1)S(1)} custom-call(s32[4,16,256]{2,1,0:T(8,128)S(1)} %copy.17.held_ref.near_ref, bf16[1024,1024]{1,0:T(8,128)(2,1)S(1)} %copy-done), custom_call_target="tpu_custom_call" | custom-call | flops 40000000 | bytes 6000000 | tf_op jit(solution)/shard_map/turn/pallas_call | solution.py:623
  15.1 0.3 %collective-permute-done.3 = s32[5,8,256]{2,1,0:T(8,128)S(1)} collective-permute-done((s32[5,8,256]{2,1,0:T(8,128)S(1)}, s32[5,8,256]{2,1,0:T(8,128)S(1)}, u32[]{:S(2)}, u32[]{:S(2)}) %collective-permute-start.3) | collective-permute-done | bytes 40992 | tf_op jit(solution)/shard_map/ppermute | solution.py:558
  15.5 0.1 collective-permute-start.4
  15.5 1.4 %spans.3 = (f32[4,1024,128]{2,1,0:T(8,128)S(1)}, f32[2,4,16,256]{3,2,1,0:T(8,128)S(1)}, f32[4,16,256]{2,1,0:T(8,128)S(1)}) custom-call(s32[8,16,256]{2,1,0:T(8,128)S(1)} %pad_add_fusion.held_ref, bf16[2,1280,128]{2,1,0:T(8,128)(2,1)S(1)} %get-tuple-element.40.conv_ref, f32[2,16,256]{2,1,0:T(8,128)S(1)} %get-tuple-element.34.rate_ref), custom_call_target="tpu_custom_call" | custom-call | flops 2000000000 | bytes 4000000 | tf_op jit(solution)/shard_map/spans/pallas_call | solution.py:605
  17.0 0.0 collective-permute-done.4.far_ref
  17.0 1.3 %combine.1 = (f32[1024,256]{1,0:T(8,128)S(1)}, bf16[1024,256]{1,0:T(8,128)(2,1)S(1)}, bf16[2,128,256]{2,1,0:T(8,128)(2,1)S(1)}) custom-call(s32[8,16,256]{2,1,0:T(8,128)S(1)} %pad_add_fusion.held_ref, s32[8,16,256]{2,1,0:T(8,128)S(1)} %collective-permute-done.4.far_ref, f32[4,1024,128]{2,1,0:T(8,128)S(1)} %get-tuple-element.45.state_a, ...), custom_call_target="tpu_custom_call" | custom-call | flops 1000000000 | bytes 8000000 | tf_op jit(solution)/shard_map/combine/pallas_call | solution.py:657
  18.3 0.6 %collective-permute-start.5 = (bf16[1024,256]{1,0:T(8,128)(2,1)S(1)}, bf16[1024,256]{1,0:T(8,128)(2,1)S(1)}, u32[]{:S(2)}, u32[]{:S(2)}) collective-permute-start(bf16[1024,256]{1,0:T(8,128)(2,1)S(1)} %get-tuple-element.52), channel_id=1, source_target_pairs={{0,1},{1,0},{2,3},{3,2},{4,5},{5,4},{6,7},{7,6},{8,9},{9,8},{10,11... | collective-permute-start | bytes 1572872 | tf_op jit(solution)/shard_map/ppermute | solution.py:558
  18.9 1.4 %own.1 = (f32[1024,256]{1,0:T(8,128)S(1)}, bf16[1024,256]{1,0:T(8,128)(2,1)S(1)}, bf16[256,256]{1,0:T(8,128)(2,1)S(1)}, bf16[2,128,256]{2,1,0:T(8,128)(2,1)S(1)}) custom-call(bf16[2,128,256]{2,1,0:T(8,128)(2,1)S(1)} %get-tuple-element.55.onehot_ref, bf16[2,1280,128]{2,1,0:T(8,128)(2,1)S(1)} %get-tuple-element.40.conv_ref, ...), custom_call_target="tpu_custom_call" | custom-call | flops 3000000000 | bytes 9000000 | tf_op jit(solution)/shard_map/own/pallas_call | solution.py:701
  20.2 0.2 collective-permute-done.5.mate_ref
  20.4 2.5 %output.1 = bf16[256,1024]{1,0:T(8,128)(2,1)} custom-call(f32[1024,256]{1,0:T(8,128)S(1)} %get-tuple-element.51.mine_ref, bf16[1024,256]{1,0:T(8,128)(2,1)S(1)} %collective-permute-done.5.mate_ref, f32[2,16,256]{2,1,0:T(8,128)S(1)} %get-tuple-element.53.reach_ref, bf16[2,16,256,256]{3,2,1,0:T(8,128)(2,1)S(1)} %get-tuple-element.54.decay_ref, ...), custom_call_target="tpu_custom_call" | custom-call | flops 2000000000 | bytes 6000000 | tf_op jit(solution)/shard_map/output/pallas_call | solution.py:715
  (14 shorter events, 0.1 us)
Async XLA Ops:
  0.8 10.3 %collective-permute-start.2 = (s32[1,16,256]{2,0,1:T(1,128)S(1)}, s32[1,16,256]{2,0,1:T(1,128)S(1)}, u32[]{:S(2)}, u32[]{:S(2)}) collective-permute-start(s32[1,16,256]{2,0,1:T(1,128)S(1)} %copy.14), channel_id=1, source_target_pairs={{0,4},{1,5},{2,6},{3,7},{4,0},{5,1},{6,2},{7,3},{8,12},{9,13},{10,... | collective-permute-start | bytes 49160 | tf_op jit(solution)/shard_map/ppermute | solution.py:558
  3.9 7.2 %collective-permute-start.1 = (s32[1,16,256]{2,0,1:T(1,128)S(1)}, s32[1,16,256]{2,0,1:T(1,128)S(1)}, u32[]{:S(2)}, u32[]{:S(2)}) collective-permute-start(s32[1,16,256]{2,0,1:T(1,128)S(1)} %copy.14), channel_id=1, source_target_pairs={{0,12},{1,13},{2,14},{3,15},{4,8},{5,9},{6,10},{7,11},{8,4},{9,5},... | collective-permute-start | bytes 49160 | tf_op jit(solution)/shard_map/ppermute | solution.py:558
  6.4 4.8 %collective-permute-start = (s32[1,16,256]{2,0,1:T(1,128)S(1)}, s32[1,16,256]{2,0,1:T(1,128)S(1)}, u32[]{:S(2)}, u32[]{:S(2)}) collective-permute-start(s32[1,16,256]{2,0,1:T(1,128)S(1)} %copy.14), channel_id=1, source_target_pairs={{0,8},{1,9},{2,10},{3,11},{4,12},{5,13},{6,14},{7,15},{8,0},{9,1},... | collective-permute-start | bytes 49160 | tf_op jit(solution)/shard_map/ppermute | solution.py:558
  11.3 4.1 %collective-permute-start.3 = (s32[5,8,256]{2,1,0:T(8,128)S(1)}, s32[5,8,256]{2,1,0:T(8,128)S(1)}, u32[]{:S(2)}, u32[]{:S(2)}) collective-permute-start(s32[5,8,256]{2,1,0:T(8,128)S(1)} %pad_add_fusion.2), channel_id=1, source_target_pairs={{0,2},{1,3},{2,0},{3,1},{4,6},{5,7},{6,4},{7,5},{8,10},{9,11},{10,... | collective-permute-start | bytes 122888 | tf_op jit(solution)/shard_map/ppermute | solution.py:558
  12.9 1.6 %copy-start = (bf16[1024,1024]{1,0:T(8,128)(2,1)S(1)}, bf16[1024,1024]{1,0:T(8,128)(2,1)}, u32[]{:S(2)}) copy-start(bf16[1024,1024]{1,0:T(8,128)(2,1)} %out_ref.1) | copy-start | bytes 6291460
  15.5 1.5 %collective-permute-start.4 = (s32[8,16,256]{2,1,0:T(8,128)S(1)}, s32[8,16,256]{2,1,0:T(8,128)S(1)}, u32[]{:S(2)}, u32[]{:S(2)}) collective-permute-start(s32[8,16,256]{2,1,0:T(8,128)S(1)} %pad_add_fusion.held_ref), channel_id=1, source_target_pairs={{0,1},{1,0},{2,3},{3,2},{4,5},{5,4},{6,7},{7,6},{8,9},{9,8},{10,11... | collective-permute-start | bytes 393224 | tf_op jit(solution)/shard_map/ppermute | solution.py:558
  18.3 2.1 %collective-permute-start.5 = (bf16[1024,256]{1,0:T(8,128)(2,1)S(1)}, bf16[1024,256]{1,0:T(8,128)(2,1)S(1)}, u32[]{:S(2)}, u32[]{:S(2)}) collective-permute-start(bf16[1024,256]{1,0:T(8,128)(2,1)S(1)} %get-tuple-element.52), channel_id=1, source_target_pairs={{0,1},{1,0},{2,3},{3,2},{4,5},{5,4},{6,7},{7,6},{8,9},{9,8},{10,11... | collective-permute-start | bytes 1572872 | tf_op jit(solution)/shard_map/ppermute | solution.py:558
